TPU v7x, 32 devices: a whole 2x2x4 slice. The times are simulated.
32 devices in a mesh: grp: 4 (over x, core), tile: 8 (over z, y).
Axes of the slice: x: 2, y: 2, z: 4, core: 2. Of those that a mesh axis runs over, the one named last changes fastest.
Arguments:
- factors: bfloat16 [4096, 128, 128], P('tile', 'grp'), may hold values from -0.09375 to 0.09375
- amplitudes: bfloat16 [512, 128, 128], P('tile', 'grp'), may hold values from -6 to 6
- tile_mask: int32 [8, 2, 2], replicated, may hold values 0 or 1
Outputs:
- residual: bfloat16 [128, 64, 512], P('tile', None, 'grp')
All inputs are finite; a program needn't handle non-finite values.
Results may differ from a plain program's by a relative error of at most 0.011.
Values may be sent and summed in bfloat16 or wider, within the bound.
No kernel may reach another device: no remote copies, remote signals or barrier semaphores. Data moves between devices by JAX's collectives and lax.ppermute only.
A program may use at most 128 MiB of HBM per device.

v0:
```python
import jax
import jax.numpy as jnp
from jax import lax
from jax.experimental import pallas as pl
from jax.experimental.pallas import tpu as pltpu
from jax.sharding import PartitionSpec as P


VB = 64
NB = 64
IJB = 64
SPLIT = (16, 24, 24)
CGROUP = 4
ROW_BLOCK = 512
VMEM_BYTES = 60 * 1024 * 1024


def integrals_kernel(*refs):
    left_ref, *piece_refs, out_ref = refs
    bs, d_part, _ = piece_refs[0].shape
    d_all = d_part * len(piece_refs)
    c_here = out_ref.shape[1] // d_all
    a_all = left_ref.shape[0] // c_here
    step = 8
    for i in range(0, bs, step):
        right = jnp.concatenate([ref[i + j] for j in range(step) for ref in piece_refs], axis=0)
        gram = lax.dot_general(
            left_ref[...], right, (((1,), (1,)), ((), ())), preferred_element_type=jnp.float32
        ).astype(jnp.bfloat16)
        for j in range(step):
            for c in range(c_here):
                out_ref[(i + j) * a_all : (i + j + 1) * a_all, c * d_all : (c + 1) * d_all] = gram[
                    c * a_all : (c + 1) * a_all, j * d_all : (j + 1) * d_all
                ]


def partial_integrals(left, pieces, c_all):
    rows, aux = left.shape
    a_all = rows // c_all
    bs, d_part, _ = pieces[0].shape
    d_all = d_part * len(pieces)
    piece_spec = pl.BlockSpec((bs, d_part, aux), lambda i: (0, 0, 0))
    return pl.pallas_call(
        integrals_kernel,
        grid=(c_all // CGROUP,),
        in_specs=[pl.BlockSpec((CGROUP * a_all, aux), lambda i: (i, 0))] + [piece_spec] * len(pieces),
        out_specs=pl.BlockSpec((bs * a_all, CGROUP * d_all), lambda i: (0, i)),
        out_shape=jax.ShapeDtypeStruct((bs * a_all, c_all * d_all), jnp.bfloat16),
        cost_estimate=pl.CostEstimate(
            flops=2 * rows * aux * bs * d_all,
            bytes_accessed=2 * (rows * aux + bs * d_all * (aux + rows)),
            transcendentals=0,
        ),
        compiler_params=pltpu.CompilerParams(vmem_limit_bytes=VMEM_BYTES),
        name="partial_integrals",
    )(left, *pieces)


def ladder_kernel(place_ref, integrals_ref, amps_ref, keep_ref, send_ref):
    high, quarter = keep_ref.shape[0], keep_ref.shape[-1]
    low = 2
    core, chip_x, near = place_ref[0], place_ref[1], place_ref[2]
    half = lax.dot_general(
        integrals_ref[...], amps_ref[...], (((1,), (1,)), ((), ())), preferred_element_type=jnp.float32
    ).astype(jnp.bfloat16)
    for h in range(high):
        slot = lax.rem(h - chip_x + high, high)
        blocks = [
            half[:, (h * low + c) * quarter : (h * low + c + 1) * quarter] for c in range(low)
        ]
        keep = jnp.where(core == 0, blocks[0], blocks[1])
        send = jnp.where(core == 0, blocks[1], blocks[0])
        if len(keep_ref.shape) == 3:
            keep_ref[slot], send_ref[slot] = keep, send
            continue
        _, inner, outer, bs, a_local, _ = keep_ref.shape
        a_all = outer * inner * a_local
        for i in range(inner):
            at = lax.rem(i - near + inner, inner)
            for b in range(bs):
                for o in range(outer):
                    row = b * a_all + (o * inner + i) * a_local
                    keep_ref[slot, at, o, b] = keep[row : row + a_local]
                    send_ref[slot, at, o, b] = send[row : row + a_local]


def ladder(place, integrals, amps, high, low, split):
    rows, inner = integrals.shape
    pairs = amps.shape[0]
    quarter = pairs // (high * low)
    block = ROW_BLOCK * 512 // max(512, pairs)
    if split[-1] % 16:
        shape, piece = (high, rows, quarter), (high, block, quarter)
        spec = pl.BlockSpec(piece, lambda i, place: (0, i, 0))
    else:
        near, far, a_local = split
        a_all = near * far * a_local
        shape = (high, near, far, rows // a_all, a_local, quarter)
        piece = (high, near, far, block // a_all, a_local, quarter)
        spec = pl.BlockSpec(piece, lambda i, place: (0, 0, 0, i, 0, 0))
    shape = jax.ShapeDtypeStruct(shape, jnp.bfloat16)
    return pl.pallas_call(
        ladder_kernel,
        grid_spec=pltpu.PrefetchScalarGridSpec(
            num_scalar_prefetch=1,
            grid=(rows // block,),
            in_specs=[
                pl.BlockSpec((block, inner), lambda i, place: (i, 0)),
                pl.BlockSpec((pairs, inner), lambda i, place: (0, 0), pipeline_mode=pl.Buffered(1)),
            ],
            out_specs=[spec, spec],
        ),
        out_shape=[shape, shape],
        cost_estimate=pl.CostEstimate(
            flops=2 * rows * inner * pairs,
            bytes_accessed=2 * (rows * inner + pairs * inner + rows * pairs),
            transcendentals=0,
        ),
        compiler_params=pltpu.CompilerParams(vmem_limit_bytes=VMEM_BYTES),
        name="ladder",
    )(place, integrals, amps)


def pick(x, index, axis):
    return lax.dynamic_index_in_dim(x, index, axis, keepdims=False)


def on_device(factors, amplitudes, tile_mask):
    aux, quarter, virtuals = factors.shape
    tiles, groups = lax.axis_size("tile"), lax.axis_size("grp")
    tile, grp = lax.axis_index("tile"), lax.axis_index("grp")
    low, inner = 2, 2
    high, outer = groups // low, tiles // inner
    core, chip_x = grp % low, grp // low
    near, far = tile % inner, tile // inner
    a_local = virtuals // tiles
    rows = amplitudes.shape[0]
    pairs = rows * tiles
    pair_quarter = pairs // groups
    f32, bf16 = jnp.float32, jnp.bfloat16
    if rows % IJB or VB % quarter or pair_quarter % IJB or VB % a_local or VB != NB:
        raise ValueError("block sizes")

    def shift(x, by_high=0, by_low=0, by_far=0, by_near=0):
        pairs_of = []
        for g in range(groups):
            for t in range(tiles):
                h, l = (g // low + by_high) % high, (g % low + by_low) % low
                o, i = (t // inner + by_far) % outer, (t % inner + by_near) % inner
                pairs_of.append((g * tiles + t, (h * low + l) * tiles + o * inner + i))
        return lax.ppermute(x, ("grp", "tile"), pairs_of)

    kept = lax.dynamic_slice_in_dim(tile_mask, tile * (rows // IJB), rows // IJB, 0)
    kept = pick(kept, grp * quarter // VB, 2).astype(bf16)[:, None, None, :, None]
    screened = amplitudes.reshape(rows // IJB, IJB, quarter, virtuals // VB, VB) * kept
    by_c = screened.reshape(rows, quarter, virtuals).transpose(2, 1, 0)
    by_c = by_c.reshape(high, low, quarter, quarter * rows)
    mine = pick(by_c, core, 1)
    theirs = shift(pick(by_c, 1 - core, 1), by_low=1)
    both = jnp.stack([mine, theirs])
    amp_pieces = []
    for k in range(high):
        part = pick(both, (chip_x + k) % high, 1)
        amp_pieces.append(shift(part, by_high=k) if k else part)

    window = factors[:, :, :NB].transpose(2, 1, 0)
    window, *amp_pieces = lax.optimization_barrier((window, *amp_pieces))

    amps = jnp.concatenate(amp_pieces).reshape(groups, quarter, quarter, rows)
    amps = amps.transpose(3, 1, 0, 2).reshape(rows, quarter * virtuals)
    amps = lax.all_gather(amps, "tile", axis=0, tiled=True)
    left = factors.reshape(aux, quarter * virtuals).T

    starts = [sum(SPLIT[:n]) for n in range(len(SPLIT))]
    owns = [window[s : s + size] for s, size in zip(starts, SPLIT)]
    others = [[shift(own, by_high=k) for k in range(1, high)] for own in owns]
    integrals = []
    for n, own in enumerate(owns):
        held = [own] + others[n]
        if n:
            *held, integrals[-1] = lax.optimization_barrier((*held, integrals[-1]))
        pieces = []
        for piece in held:
            pieces += [piece, shift(piece, by_low=1)]
        integrals.append(partial_integrals(left, pieces, quarter))
    amps, *integrals = lax.optimization_barrier((amps, *integrals))

    place = jnp.stack([core, chip_x, near]).astype(jnp.int32)
    chunks = []
    for n, size in enumerate(SPLIT):
        keep, send = ladder(place, integrals[n], amps, high, low, (inner, outer, a_local))
        got = shift(send, by_low=1)
        parts = []
        for kx in range(high):
            for ky in range(inner):
                if keep.ndim == 6:
                    halves = [half[kx, ky] for half in (keep, got)]
                else:
                    view = (high, size, outer, inner, a_local, pair_quarter)
                    halves = [
                        pick(half.reshape(view)[kx], (near + ky) % inner, 2).swapaxes(0, 1)
                        for half in (keep, got)
                    ]
                parts.append((halves[0].astype(f32) + halves[1].astype(f32)).astype(bf16))
        if n + 1 < len(SPLIT):
            amps, *parts = lax.optimization_barrier((amps, *parts))
        total = None
        for kx in range(high):
            for ky in range(inner):
                part = parts[kx * inner + ky]
                if kx or ky:
                    part = shift(part, by_high=kx, by_near=ky)
                total = part.astype(f32) if total is None else total + part.astype(f32)
        total = total.astype(bf16)
        done = None
        for kz in range(outer):
            part = pick(total, (far + kz) % outer, 0)
            if kz:
                part = shift(part, by_far=kz)
            done = part.astype(f32) if done is None else done + part.astype(f32)
        chunks.append(done.transpose(1, 0, 2))
    summed = jnp.concatenate(chunks, axis=1)

    blocks = pair_quarter // IJB
    shown = lax.dynamic_slice_in_dim(tile_mask, grp * blocks, blocks, 0)[:, :, 0]
    shown = pick(shown, tile * a_local // VB, 1)
    shown = jnp.broadcast_to(shown[:, None], (blocks, IJB)).reshape(pair_quarter)
    return (summed * shown.astype(f32)).astype(bf16)


def solution(mesh):
    placed = (P("tile", "grp", None), P("tile", "grp", None), P())

    return jax.shard_map(
        on_device, mesh=mesh, in_specs=placed, out_specs=P("tile", None, "grp"), check_vma=False
    )
```

profile of v0, /device:TPU:0, one launch (start us, length us, event | category | flops | bytes accessed | tf_op | source)
XLA Modules:
  0.0 259.0 jit_solution(12587055362093303189)
XLA Ops:
  6.5 0.9 fusion.30
  7.6 1.1 multiply_bitcast_fusion
  8.6 1.7 copy.8
  10.3 0.8 reshape.96
  11.8 1.2 collective-permute-done
  13.0 2.9 %collective-permute-start.1 = (bf16[2,32,2048]{2,1,0:T(8,128)(2,1)S(1)}, bf16[2,32,2048]{2,1,0:T(8,128)(2,1)S(1)}, u32[]{:S(2)}, u32[]{:S(2)}) collective-permute-start(bf16[2,32,2048]{2,1,0:T(8,128)(2,1)S(1)} %get-tuple-element.76), channel_id=1, source_target_pairs={{0,16},{1,17},{2,18},{3,19},{4,20},{5,21},{6,22},{7,23},{8,24},{9,... | collective-permute-start | bytes 786440 | tf_op jit(solution)/shard_map/ppermute | solution.py:151
  15.9 5.8 %copy.13 = bf16[512,32,64]{0,1,2:T(8,128)(2,1)S(1)} copy(bf16[512,32,64]{2,1,0:T(8,128)(2,1)} %bitcast.83) | data formatting | bytes 4194304
  21.7 0.8 collective-permute-done.1
  22.5 0.8 pad_maximum_fusion
  23.3 2.1 reshape.97
  25.4 1.1 copy.9
  26.5 2.4 copy.10
  29.0 1.8 collective-permute-start.4
  30.8 11.8 %collective-permute-done.4.refs_3_ = bf16[16,32,512]{2,1,0:T(8,128)(2,1)} collective-permute-done((bf16[16,32,512]{2,1,0:T(8,128)(2,1)S(1)}, bf16[16,32,512]{2,1,0:T(8,128)(2,1)}, u32[]{:S(2)}, u32[]{:S(2)}) %collective-permute-start.4) | collective-permute-done | bytes 524320 | tf_op jit(solution)/shard_map/ppermute | solution.py:151
  42.6 7.6 %copy.11 = bf16[512,32,128]{0,2,1:T(8,128)(2,1)} copy(bf16[512,32,128]{2,1,0:T(8,128)(2,1)} %param.3) | data formatting | bytes 8388608 | tf_op args[0]
  50.2 1.0 fusion.33
  51.2 1.5 collective-permute-start.2
  52.7 14.0 %partial_integrals.3.integrals_ref = bf16[2048,4096]{1,0:T(8,128)(2,1)} custom-call(bf16[4096,512]{1,0:T(8,128)(2,1)} %bitcast.86, bf16[16,32,512]{2,1,0:T(8,128)(2,1)} %copy-done.3, bf16[16,32,512]{2,1,0:T(8,128)(2,1)} %collective-permute-done.3.refs_2_, bf16[16,32,512]{2,1,0:T(8,128)(2,1)} %collective-permute-done.4.refs_3_, ...), custom_call_target="tpu_custom_call" | custom-call | flops 8589934592 | bytes 23068672 | tf_op jit(solution)/shard_map/partial_integrals/pallas_call | solution.py:43
  66.7 4.7 %collective-permute-done.2.refs_3_ = bf16[24,32,512]{2,1,0:T(8,128)(2,1)S(1)} collective-permute-done((bf16[24,32,512]{2,1,0:T(8,128)(2,1)}, bf16[24,32,512]{2,1,0:T(8,128)(2,1)S(1)}, u32[]{:S(2)}, u32[]{:S(2)}) %collective-permute-start.2) | collective-permute-done | bytes 786464 | tf_op jit(solution)/shard_map/ppermute | solution.py:151
  71.9 1.5 collective-permute-start.6
  73.4 0.7 collective-permute-done.7.refs_2_
  74.0 1.1 collective-permute-done.8.refs_4_
  75.1 18.6 %partial_integrals.4.integrals_ref = bf16[3072,4096]{1,0:T(8,128)(2,1)} custom-call(bf16[4096,512]{1,0:T(8,128)(2,1)} %bitcast.87, bf16[24,32,512]{2,1,0:T(8,128)(2,1)} %get-tuple-element.38.refs_1_, bf16[24,32,512]{2,1,0:T(8,128)(2,1)} %collective-permute-done.7.refs_2_, bf16[24,32,512]{2,1,0:T(8,128)(2,1)} %copy-done.5, ...), custom_call_target="tpu_custom_call" | custom-call | flops 12884901888 | bytes 32505856 | tf_op jit(solution)/shard_map/partial_integrals/pallas_call | solution.py:43
  94.3 0.6 pad_add_fusion.place_ref
  94.9 1.2 collective-permute-done.10.refs_4_
  96.1 1.3 collective-permute-done.9.refs_2_
  97.4 18.6 %partial_integrals.5.integrals_ref = bf16[3072,4096]{1,0:T(8,128)(2,1)} custom-call(bf16[4096,512]{1,0:T(8,128)(2,1)} %bitcast.88, bf16[24,32,512]{2,1,0:T(8,128)(2,1)} %copy-done.2, bf16[24,32,512]{2,1,0:T(8,128)(2,1)} %collective-permute-done.9.refs_2_, bf16[24,32,512]{2,1,0:T(8,128)(2,1)} %copy-done.4, bf16[24,32,512]{2,1,0:T(8,128)(2,1)} %copy-done.6), custom_call_target="tpu_custom_call" | custom-call | flops 12884901888 | bytes 32505856 | tf_op jit(solution)/shard_map/partial_integrals/pallas_call | solution.py:43
  116.0 14.7 %ladder.3 = (bf16[2,2,4,16,16,128]{5,4,3,2,1,0:T(8,128)(2,1)}, bf16[2,2,4,16,16,128]{5,4,3,2,1,0:T(8,128)(2,1)}) custom-call(s32[3]{0:T(128)} %pad_add_fusion.place_ref, bf16[2048,4096]{1,0:T(8,128)(2,1)} %partial_integrals.3.integrals_ref, bf16[512,4096]{1,0:T(8,128)(2,1)} %all-gather.2.cloned.1.call-done.amps_ref), custom_call_target="tpu_custom_call" | custom-call | flops 8589934592 | bytes 23068672 | tf_op jit(solution)/shard_map/ladder/pallas_call | solution.py:102
  130.8 2.7 %collective-permute-done.11 = bf16[2,2,4,16,16,128]{5,4,3,2,1,0:T(8,128)(2,1)S(1)} collective-permute-done((bf16[2,2,4,16,16,128]{5,4,3,2,1,0:T(8,128)(2,1)}, bf16[2,2,4,16,16,128]{5,4,3,2,1,0:T(8,128)(2,1)S(1)}, u32[]{:S(2)}, u32[]{:S(2)}) %collective-permute-start.11) | collective-permute-done | bytes 1048608 | tf_op jit(solution)/shard_map/ppermute | solution.py:151
  133.5 2.3 fusion.15
  135.9 19.6 %ladder.4 = (bf16[2,2,4,24,16,128]{5,4,3,2,1,0:T(8,128)(2,1)}, bf16[2,2,4,24,16,128]{5,4,3,2,1,0:T(8,128)(2,1)}) custom-call(s32[3]{0:T(128)} %pad_add_fusion.place_ref, bf16[3072,4096]{1,0:T(8,128)(2,1)} %partial_integrals.4.integrals_ref, bf16[512,4096]{1,0:T(8,128)(2,1)} %all-gather.2.cloned.1.call-done.amps_ref), custom_call_target="tpu_custom_call" | custom-call | flops 12884901888 | bytes 32505856 | tf_op jit(solution)/shard_map/ladder/pallas_call | solution.py:102
  155.6 3.5 %collective-permute-done.18 = bf16[2,2,4,24,16,128]{5,4,3,2,1,0:T(8,128)(2,1)S(1)} collective-permute-done((bf16[2,2,4,24,16,128]{5,4,3,2,1,0:T(8,128)(2,1)}, bf16[2,2,4,24,16,128]{5,4,3,2,1,0:T(8,128)(2,1)S(1)}, u32[]{:S(2)}, u32[]{:S(2)}) %collective-permute-start.18) | collective-permute-done | bytes 1572896 | tf_op jit(solution)/shard_map/ppermute | solution.py:151
  159.1 2.7 %fusion.7 = (bf16[4,24,16,128]{3,2,1,0:T(8,128)(2,1)}, bf16[4,24,16,128]{3,2,1,0:T(8,128)(2,1)}, bf16[4,24,16,128]{3,2,1,0:T(8,128)(2,1)}, bf16[4,24,16,128]{3,2,1,0:T(8,128)(2,1)S(1)}) fusion(bf16[2,2,4,24,16,128]{5,4,3,2,1,0:T(8,128)(2,1)S(1)} %collective-permute-done.18, bf16[2,2,4,24,16,128]{5,4,3,2,1,0:T(8,128)(2,1)} %get-tuple-element.53), kind=kLoop, calls=%fused_computation.29 | loop fusion | flops 3145728 | bytes 4718592 | tf_op jit(solution)/shard_map/convert_element_type | solution.py:204
  161.8 19.6 %ladder.5 = (bf16[2,2,4,24,16,128]{5,4,3,2,1,0:T(8,128)(2,1)}, bf16[2,2,4,24,16,128]{5,4,3,2,1,0:T(8,128)(2,1)}) custom-call(s32[3]{0:T(128)} %pad_add_fusion.place_ref, bf16[3072,4096]{1,0:T(8,128)(2,1)} %partial_integrals.5.integrals_ref, bf16[512,4096]{1,0:T(8,128)(2,1)} %all-gather.2.cloned.1.call-done.amps_ref), custom_call_target="tpu_custom_call" | custom-call | flops 12884901888 | bytes 32505856 | tf_op jit(solution)/shard_map/ladder/pallas_call | solution.py:102
  181.5 1.5 collective-permute-start.12
  183.0 1.5 collective-permute-start.13
  185.0 5.4 %collective-permute-done.12 = bf16[4,16,16,128]{3,2,1,0:T(8,128)(2,1)} collective-permute-done((bf16[4,16,16,128]{3,2,1,0:T(8,128)(2,1)}, bf16[4,16,16,128]{3,2,1,0:T(8,128)(2,1)}, u32[]{:S(2)}, u32[]{:S(2)}) %collective-permute-start.12) | collective-permute-done | bytes 262176 | tf_op jit(solution)/shard_map/ppermute | solution.py:151
  190.4 2.1 collective-permute-done.13
  192.5 4.7 %collective-permute-done.14 = bf16[4,16,16,128]{3,2,1,0:T(8,128)(2,1)} collective-permute-done((bf16[4,16,16,128]{3,2,1,0:T(8,128)(2,1)}, bf16[4,16,16,128]{3,2,1,0:T(8,128)(2,1)}, u32[]{:S(2)}, u32[]{:S(2)}) %collective-permute-start.14) | collective-permute-done | bytes 262176 | tf_op jit(solution)/shard_map/ppermute | solution.py:151
  197.2 1.3 add_convert_fusion.9
  198.5 0.7 copy-done.1
  199.2 0.7 dynamic-slice_bitcast_fusion.10
  199.9 1.6 collective-permute-start.15
  201.5 2.6 collective-permute-start.16
  204.0 1.4 collective-permute-start.17
  205.4 0.8 fusion.32
  206.3 1.5 collective-permute-start.19
  207.8 1.5 collective-permute-start.20
  209.3 2.0 collective-permute-start.21
  211.4 1.0 fusion.28
  213.3 1.0 collective-permute-start.27
  214.3 11.0 %collective-permute-done.19 = bf16[4,24,16,128]{3,2,1,0:T(8,128)(2,1)S(1)} collective-permute-done((bf16[4,24,16,128]{3,2,1,0:T(8,128)(2,1)}, bf16[4,24,16,128]{3,2,1,0:T(8,128)(2,1)S(1)}, u32[]{:S(2)}, u32[]{:S(2)}) %collective-permute-start.19) | collective-permute-done | bytes 393248 | tf_op jit(solution)/shard_map/ppermute | solution.py:151
  225.3 2.6 collective-permute-start.28
  227.9 0.7 collective-permute-done.21
  229.4 1.2 collective-permute-start.23
  230.6 4.0 %collective-permute-done.26 = bf16[4,24,16,128]{3,2,1,0:T(8,128)(2,1)S(1)} collective-permute-done((bf16[4,24,16,128]{3,2,1,0:T(8,128)(2,1)S(1)}, bf16[4,24,16,128]{3,2,1,0:T(8,128)(2,1)S(1)}, u32[]{:S(2)}, u32[]{:S(2)}) %collective-permute-start.26) | collective-permute-done | bytes 393248 | tf_op jit(solution)/shard_map/ppermute | solution.py:151
  234.6 2.4 collective-permute-done.27
  236.9 5.5 %collective-permute-done.28 = bf16[4,24,16,128]{3,2,1,0:T(8,128)(2,1)S(1)} collective-permute-done((bf16[4,24,16,128]{3,2,1,0:T(8,128)(2,1)S(1)}, bf16[4,24,16,128]{3,2,1,0:T(8,128)(2,1)S(1)}, u32[]{:S(2)}, u32[]{:S(2)}) %collective-permute-start.28) | collective-permute-done | bytes 393248 | tf_op jit(solution)/shard_map/ppermute | solution.py:151
  242.8 0.7 collective-permute-start.29
  243.5 1.1 collective-permute-start.30
  244.6 2.0 collective-permute-start.31
  246.7 2.7 %collective-permute-done.29 = bf16[24,16,128]{2,1,0:T(8,128)(2,1)S(1)} collective-permute-done((bf16[24,16,128]{2,1,0:T(8,128)(2,1)S(1)}, bf16[24,16,128]{2,1,0:T(8,128)(2,1)S(1)}, u32[]{:S(2)}, u32[]{:S(2)}) %collective-permute-start.29) | collective-permute-done | bytes 98336 | tf_op jit(solution)/shard_map/ppermute | solution.py:151
  249.4 1.9 collective-permute-done.30
  251.4 0.8 copy.12
  (57 shorter events, 5.3 us)
Async XLA Ops:
  6.5 109.4 %all-gather.2.cloned.1.call-start = ((), (), s32[]{:S(2)}) async-start(), calls=%async_computation | async-start | bytes 4718592 | tf_op jit(solution)/shard_map/all_gather | solution.py:171
  11.2 1.7 collective-permute-start
  13.0 9.5 %collective-permute-start.1 = (bf16[2,32,2048]{2,1,0:T(8,128)(2,1)S(1)}, bf16[2,32,2048]{2,1,0:T(8,128)(2,1)S(1)}, u32[]{:S(2)}, u32[]{:S(2)}) collective-permute-start(bf16[2,32,2048]{2,1,0:T(8,128)(2,1)S(1)} %get-tuple-element.76), channel_id=1, source_target_pairs={{0,16},{1,17},{2,18},{3,19},{4,20},{5,21},{6,22},{7,23},{8,24},{9,... | collective-permute-start | bytes 786440 | tf_op jit(solution)/shard_map/ppermute | solution.py:151
  29.0 21.2 %copy-start.3 = (bf16[16,32,512]{2,1,0:T(8,128)(2,1)}, bf16[16,32,512]{2,1,0:T(8,128)(2,1)S(1)}, u32[]{:S(2)}) copy-start(bf16[16,32,512]{2,1,0:T(8,128)(2,1)S(1)} %slice.89.refs_1_) | copy-start | bytes 1572868
  29.0 13.6 %collective-permute-start.4 = (bf16[16,32,512]{2,1,0:T(8,128)(2,1)S(1)}, bf16[16,32,512]{2,1,0:T(8,128)(2,1)}, u32[]{:S(2)}, u32[]{:S(2)}) collective-permute-start(bf16[16,32,512]{2,1,0:T(8,128)(2,1)S(1)} %slice.89.refs_1_), channel_id=1, source_target_pairs={{0,16},{1,17},{2,18},{3,19},{4,20},{5,21},{6,22},{7,23},{8,24},{9,... | collective-permute-start | bytes 1572872 | tf_op jit(solution)/shard_map/ppermute | solution.py:151
  30.8 21.9 %collective-permute-start.3 = (bf16[16,32,512]{2,1,0:T(8,128)(2,1)S(1)}, bf16[16,32,512]{2,1,0:T(8,128)(2,1)}, u32[]{:S(2)}, u32[]{:S(2)}) collective-permute-start(bf16[16,32,512]{2,1,0:T(8,128)(2,1)S(1)} %slice.89.refs_1_), channel_id=1, source_target_pairs={{0,8},{1,9},{2,10},{3,11},{4,12},{5,13},{6,14},{7,15},{8,0},{9,1},... | collective-permute-start | bytes 1572872 | tf_op jit(solution)/shard_map/ppermute | solution.py:151
  42.6 10.1 %collective-permute-start.5 = (bf16[16,32,512]{2,1,0:T(8,128)(2,1)}, bf16[16,32,512]{2,1,0:T(8,128)(2,1)}, u32[]{:S(2)}, u32[]{:S(2)}) collective-permute-start(bf16[16,32,512]{2,1,0:T(8,128)(2,1)} %collective-permute-done.4.refs_3_), channel_id=1, source_target_pairs={{0,8},{1,9},{2,10},{3,11},{4,12},{5,13},{6,14},{7,15},{8,0},{9,1},... | collective-permute-start | bytes 1572872 | tf_op jit(solution)/shard_map/ppermute | solution.py:151
  51.2 42.7 %copy-start.2 = (bf16[24,32,512]{2,1,0:T(8,128)(2,1)}, bf16[24,32,512]{2,1,0:T(8,128)(2,1)S(1)}, u32[]{:S(2)}) copy-start(bf16[24,32,512]{2,1,0:T(8,128)(2,1)S(1)} %get-tuple-element.41.refs_1_) | copy-start | bytes 2359300
  51.2 20.2 %collective-permute-start.2 = (bf16[24,32,512]{2,1,0:T(8,128)(2,1)}, bf16[24,32,512]{2,1,0:T(8,128)(2,1)S(1)}, u32[]{:S(2)}, u32[]{:S(2)}) collective-permute-start(bf16[24,32,512]{2,1,0:T(8,128)(2,1)} %get-tuple-element.38.refs_1_), channel_id=1, source_target_pairs={{0,16},{1,17},{2,18},{3,19},{4,20},{5,21},{6,22},{7,23},{8,24},{9,... | collective-permute-start | bytes 2359304 | tf_op jit(solution)/shard_map/ppermute | solution.py:151
  71.4 3.8 %copy-start.5 = (bf16[24,32,512]{2,1,0:T(8,128)(2,1)}, bf16[24,32,512]{2,1,0:T(8,128)(2,1)S(1)}, u32[]{:S(2)}) copy-start(bf16[24,32,512]{2,1,0:T(8,128)(2,1)S(1)} %collective-permute-done.2.refs_3_) | copy-start | bytes 2359300
  71.4 2.6 %collective-permute-start.7 = (bf16[24,32,512]{2,1,0:T(8,128)(2,1)}, bf16[24,32,512]{2,1,0:T(8,128)(2,1)}, u32[]{:S(2)}, u32[]{:S(2)}) collective-permute-start(bf16[24,32,512]{2,1,0:T(8,128)(2,1)} %get-tuple-element.38.refs_1_), channel_id=1, source_target_pairs={{0,8},{1,9},{2,10},{3,11},{4,12},{5,13},{6,14},{7,15},{8,0},{9,1},... | collective-permute-start | bytes 2359304 | tf_op jit(solution)/shard_map/ppermute | solution.py:151
  71.4 3.7 %collective-permute-start.8 = (bf16[24,32,512]{2,1,0:T(8,128)(2,1)S(1)}, bf16[24,32,512]{2,1,0:T(8,128)(2,1)}, u32[]{:S(2)}, u32[]{:S(2)}) collective-permute-start(bf16[24,32,512]{2,1,0:T(8,128)(2,1)S(1)} %collective-permute-done.2.refs_3_), channel_id=1, source_target_pairs={{0,8},{1,9},{2,10},{3,11},{4,12},{5,13},{6,14},{7,15},{8,0},{9,1},... | collective-permute-start | bytes 2359304 | tf_op jit(solution)/shard_map/ppermute | solution.py:151
  71.9 21.8 %collective-permute-start.6 = (bf16[24,32,512]{2,1,0:T(8,128)(2,1)S(1)}, bf16[24,32,512]{2,1,0:T(8,128)(2,1)S(1)}, u32[]{:S(2)}, u32[]{:S(2)}) collective-permute-start(bf16[24,32,512]{2,1,0:T(8,128)(2,1)S(1)} %get-tuple-element.41.refs_1_), channel_id=1, source_target_pairs={{0,16},{1,17},{2,18},{3,19},{4,20},{5,21},{6,22},{7,23},{8,24},{9,... | collective-permute-start | bytes 2359304 | tf_op jit(solution)/shard_map/ppermute | solution.py:151
  93.7 3.6 %copy-start.4 = (bf16[24,32,512]{2,1,0:T(8,128)(2,1)}, bf16[24,32,512]{2,1,0:T(8,128)(2,1)S(1)}, u32[]{:S(2)}) copy-start(bf16[24,32,512]{2,1,0:T(8,128)(2,1)S(1)} %collective-permute-done.6.refs_3_) | copy-start | bytes 2359300
  93.7 2.4 collective-permute-start.10
  93.9 3.4 %collective-permute-start.9 = (bf16[24,32,512]{2,1,0:T(8,128)(2,1)S(1)}, bf16[24,32,512]{2,1,0:T(8,128)(2,1)}, u32[]{:S(2)}, u32[]{:S(2)}) collective-permute-start(bf16[24,32,512]{2,1,0:T(8,128)(2,1)S(1)} %get-tuple-element.41.refs_1_), channel_id=1, source_target_pairs={{0,8},{1,9},{2,10},{3,11},{4,12},{5,13},{6,14},{7,15},{8,0},{9,1},... | collective-permute-start | bytes 2359304 | tf_op jit(solution)/shard_map/ppermute | solution.py:151
  96.1 1.3 copy-start.6
  130.7 2.9 %collective-permute-start.11 = (bf16[2,2,4,16,16,128]{5,4,3,2,1,0:T(8,128)(2,1)}, bf16[2,2,4,16,16,128]{5,4,3,2,1,0:T(8,128)(2,1)S(1)}, u32[]{:S(2)}, u32[]{:S(2)}) collective-permute-start(bf16[2,2,4,16,16,128]{5,4,3,2,1,0:T(8,128)(2,1)} %get-tuple-element.46), channel_id=1, source_target_pairs={{0,8},{1,9},{2,10},{3,11},{4,12},{5,13},{6,14},{7,15},{8,0},{9,1},... | collective-permute-start | bytes 3145736 | tf_op jit(solution)/shard_map/ppermute | solution.py:151
  155.5 3.6 %collective-permute-start.18 = (bf16[2,2,4,24,16,128]{5,4,3,2,1,0:T(8,128)(2,1)}, bf16[2,2,4,24,16,128]{5,4,3,2,1,0:T(8,128)(2,1)S(1)}, u32[]{:S(2)}, u32[]{:S(2)}) collective-permute-start(bf16[2,2,4,24,16,128]{5,4,3,2,1,0:T(8,128)(2,1)} %get-tuple-element.54), channel_id=1, source_target_pairs={{0,8},{1,9},{2,10},{3,11},{4,12},{5,13},{6,14},{7,15},{8,0},{9,1},... | collective-permute-start | bytes 4718600 | tf_op jit(solution)/shard_map/ppermute | solution.py:151
  181.4 31.0 %copy-start = (bf16[2,2,4,24,16,128]{5,4,3,2,1,0:T(8,128)(2,1)S(1)}, bf16[2,2,4,24,16,128]{5,4,3,2,1,0:T(8,128)(2,1)}, u32[]{:S(2)}) copy-start(bf16[2,2,4,24,16,128]{5,4,3,2,1,0:T(8,128)(2,1)} %get-tuple-element.61) | copy-start | bytes 4718596
  181.4 31.0 %collective-permute-start.25 = (bf16[2,2,4,24,16,128]{5,4,3,2,1,0:T(8,128)(2,1)}, bf16[2,2,4,24,16,128]{5,4,3,2,1,0:T(8,128)(2,1)S(1)}, u32[]{:S(2)}, u32[]{:S(2)}) collective-permute-start(bf16[2,2,4,24,16,128]{5,4,3,2,1,0:T(8,128)(2,1)} %get-tuple-element.62), channel_id=1, source_target_pairs={{0,8},{1,9},{2,10},{3,11},{4,12},{5,13},{6,14},{7,15},{8,0},{9,1},... | collective-permute-start | bytes 4718600 | tf_op jit(solution)/shard_map/ppermute | solution.py:151
  181.5 8.9 %collective-permute-start.12 = (bf16[4,16,16,128]{3,2,1,0:T(8,128)(2,1)}, bf16[4,16,16,128]{3,2,1,0:T(8,128)(2,1)}, u32[]{:S(2)}, u32[]{:S(2)}) collective-permute-start(bf16[4,16,16,128]{3,2,1,0:T(8,128)(2,1)} %get-tuple-element.48), channel_id=1, source_target_pairs={{0,1},{1,0},{2,3},{3,2},{4,5},{5,4},{6,7},{7,6},{8,9},{9,8},{10,11... | collective-permute-start | bytes 786440 | tf_op jit(solution)/shard_map/ppermute | solution.py:151
  183.0 9.5 %collective-permute-start.13 = (bf16[4,16,16,128]{3,2,1,0:T(8,128)(2,1)}, bf16[4,16,16,128]{3,2,1,0:T(8,128)(2,1)}, u32[]{:S(2)}, u32[]{:S(2)}) collective-permute-start(bf16[4,16,16,128]{3,2,1,0:T(8,128)(2,1)} %get-tuple-element.49), channel_id=1, source_target_pairs={{0,16},{1,17},{2,18},{3,19},{4,20},{5,21},{6,22},{7,23},{8,24},{9,... | collective-permute-start | bytes 786440 | tf_op jit(solution)/shard_map/ppermute | solution.py:151
  184.5 12.7 %collective-permute-start.14 = (bf16[4,16,16,128]{3,2,1,0:T(8,128)(2,1)}, bf16[4,16,16,128]{3,2,1,0:T(8,128)(2,1)}, u32[]{:S(2)}, u32[]{:S(2)}) collective-permute-start(bf16[4,16,16,128]{3,2,1,0:T(8,128)(2,1)} %get-tuple-element.50), channel_id=1, source_target_pairs={{0,17},{1,16},{2,19},{3,18},{4,21},{5,20},{6,23},{7,22},{8,25},{9,... | collective-permute-start | bytes 786440 | tf_op jit(solution)/shard_map/ppermute | solution.py:151
  198.5 0.7 copy-start.1
  199.9 7.9 %collective-permute-start.15 = (bf16[16,16,128]{2,1,0:T(8,128)(2,1)}, bf16[16,16,128]{2,1,0:T(8,128)(2,1)}, u32[]{:S(2)}, u32[]{:S(2)}) collective-permute-start(bf16[16,16,128]{2,1,0:T(8,128)(2,1)} %get-tuple-element.86), channel_id=1, source_target_pairs={{0,2},{1,3},{2,4},{3,5},{4,6},{5,7},{6,0},{7,1},{8,10},{9,11},{10,... | collective-permute-start | bytes 196616 | tf_op jit(solution)/shard_map/ppermute | solution.py:151
  201.5 7.9 %collective-permute-start.16 = (bf16[16,16,128]{2,1,0:T(8,128)(2,1)}, bf16[16,16,128]{2,1,0:T(8,128)(2,1)}, u32[]{:S(2)}, u32[]{:S(2)}) collective-permute-start(bf16[16,16,128]{2,1,0:T(8,128)(2,1)} %get-tuple-element.88), channel_id=1, source_target_pairs={{0,4},{1,5},{2,6},{3,7},{4,0},{5,1},{6,2},{7,3},{8,12},{9,13},{10,... | collective-permute-start | bytes 196616 | tf_op jit(solution)/shard_map/ppermute | solution.py:151
  204.0 7.3 %collective-permute-start.17 = (bf16[16,16,128]{2,1,0:T(8,128)(2,1)}, bf16[16,16,128]{2,1,0:T(8,128)(2,1)}, u32[]{:S(2)}, u32[]{:S(2)}) collective-permute-start(bf16[16,16,128]{2,1,0:T(8,128)(2,1)} %get-tuple-element.87), channel_id=1, source_target_pairs={{0,6},{1,7},{2,0},{3,1},{4,2},{5,3},{6,4},{7,5},{8,14},{9,15},{10,... | collective-permute-start | bytes 196616 | tf_op jit(solution)/shard_map/ppermute | solution.py:151
  206.3 19.0 %collective-permute-start.19 = (bf16[4,24,16,128]{3,2,1,0:T(8,128)(2,1)}, bf16[4,24,16,128]{3,2,1,0:T(8,128)(2,1)S(1)}, u32[]{:S(2)}, u32[]{:S(2)}) collective-permute-start(bf16[4,24,16,128]{3,2,1,0:T(8,128)(2,1)} %get-tuple-element.56), channel_id=1, source_target_pairs={{0,1},{1,0},{2,3},{3,2},{4,5},{5,4},{6,7},{7,6},{8,9},{9,8},{10,11... | collective-permute-start | bytes 1179656 | tf_op jit(solution)/shard_map/ppermute | solution.py:151
  207.8 20.0 %collective-permute-start.20 = (bf16[4,24,16,128]{3,2,1,0:T(8,128)(2,1)}, bf16[4,24,16,128]{3,2,1,0:T(8,128)(2,1)S(1)}, u32[]{:S(2)}, u32[]{:S(2)}) collective-permute-start(bf16[4,24,16,128]{3,2,1,0:T(8,128)(2,1)} %get-tuple-element.57), channel_id=1, source_target_pairs={{0,16},{1,17},{2,18},{3,19},{4,20},{5,21},{6,22},{7,23},{8,24},{9,... | collective-permute-start | bytes 1179656 | tf_op jit(solution)/shard_map/ppermute | solution.py:151
  209.3 19.2 %collective-permute-start.21 = (bf16[4,24,16,128]{3,2,1,0:T(8,128)(2,1)}, bf16[4,24,16,128]{3,2,1,0:T(8,128)(2,1)S(1)}, u32[]{:S(2)}, u32[]{:S(2)}) collective-permute-start(bf16[4,24,16,128]{3,2,1,0:T(8,128)(2,1)} %get-tuple-element.58), channel_id=1, source_target_pairs={{0,17},{1,16},{2,19},{3,18},{4,21},{5,20},{6,23},{7,22},{8,25},{9,... | collective-permute-start | bytes 1179656 | tf_op jit(solution)/shard_map/ppermute | solution.py:151
  212.7 21.8 %collective-permute-start.26 = (bf16[4,24,16,128]{3,2,1,0:T(8,128)(2,1)S(1)}, bf16[4,24,16,128]{3,2,1,0:T(8,128)(2,1)S(1)}, u32[]{:S(2)}, u32[]{:S(2)}) collective-permute-start(bf16[4,24,16,128]{3,2,1,0:T(8,128)(2,1)S(1)} %get-tuple-element.63), channel_id=1, source_target_pairs={{0,1},{1,0},{2,3},{3,2},{4,5},{5,4},{6,7},{7,6},{8,9},{9,8},{10,11... | collective-permute-start | bytes 1179656 | tf_op jit(solution)/shard_map/ppermute | solution.py:151
  213.3 23.6 %collective-permute-start.27 = (bf16[4,24,16,128]{3,2,1,0:T(8,128)(2,1)S(1)}, bf16[4,24,16,128]{3,2,1,0:T(8,128)(2,1)S(1)}, u32[]{:S(2)}, u32[]{:S(2)}) collective-permute-start(bf16[4,24,16,128]{3,2,1,0:T(8,128)(2,1)S(1)} %get-tuple-element.65), channel_id=1, source_target_pairs={{0,16},{1,17},{2,18},{3,19},{4,20},{5,21},{6,22},{7,23},{8,24},{9,... | collective-permute-start | bytes 1179656 | tf_op jit(solution)/shard_map/ppermute | solution.py:151
  225.3 17.2 %collective-permute-start.28 = (bf16[4,24,16,128]{3,2,1,0:T(8,128)(2,1)S(1)}, bf16[4,24,16,128]{3,2,1,0:T(8,128)(2,1)S(1)}, u32[]{:S(2)}, u32[]{:S(2)}) collective-permute-start(bf16[4,24,16,128]{3,2,1,0:T(8,128)(2,1)S(1)} %get-tuple-element.64), channel_id=1, source_target_pairs={{0,17},{1,16},{2,19},{3,18},{4,21},{5,20},{6,23},{7,22},{8,25},{9,... | collective-permute-start | bytes 1179656 | tf_op jit(solution)/shard_map/ppermute | solution.py:151
  228.9 15.8 %collective-permute-start.22 = (bf16[24,16,128]{2,1,0:T(8,128)(2,1)S(1)}, bf16[24,16,128]{2,1,0:T(8,128)(2,1)S(1)}, u32[]{:S(2)}, u32[]{:S(2)}) collective-permute-start(bf16[24,16,128]{2,1,0:T(8,128)(2,1)S(1)} %get-tuple-element.80), channel_id=1, source_target_pairs={{0,2},{1,3},{2,4},{3,5},{4,6},{5,7},{6,0},{7,1},{8,10},{9,11},{10,... | collective-permute-start | bytes 294920 | tf_op jit(solution)/shard_map/ppermute | solution.py:151
  229.4 17.2 %collective-permute-start.23 = (bf16[24,16,128]{2,1,0:T(8,128)(2,1)S(1)}, bf16[24,16,128]{2,1,0:T(8,128)(2,1)S(1)}, u32[]{:S(2)}, u32[]{:S(2)}) collective-permute-start(bf16[24,16,128]{2,1,0:T(8,128)(2,1)S(1)} %get-tuple-element.82), channel_id=1, source_target_pairs={{0,4},{1,5},{2,6},{3,7},{4,0},{5,1},{6,2},{7,3},{8,12},{9,13},{10,... | collective-permute-start | bytes 294920 | tf_op jit(solution)/shard_map/ppermute | solution.py:151
  234.6 12.1 %collective-permute-start.24 = (bf16[24,16,128]{2,1,0:T(8,128)(2,1)S(1)}, bf16[24,16,128]{2,1,0:T(8,128)(2,1)S(1)}, u32[]{:S(2)}, u32[]{:S(2)}) collective-permute-start(bf16[24,16,128]{2,1,0:T(8,128)(2,1)S(1)} %get-tuple-element.81), channel_id=1, source_target_pairs={{0,6},{1,7},{2,0},{3,1},{4,2},{5,3},{6,4},{7,5},{8,14},{9,15},{10,... | collective-permute-start | bytes 294920 | tf_op jit(solution)/shard_map/ppermute | solution.py:151
  242.8 6.6 %collective-permute-start.29 = (bf16[24,16,128]{2,1,0:T(8,128)(2,1)S(1)}, bf16[24,16,128]{2,1,0:T(8,128)(2,1)S(1)}, u32[]{:S(2)}, u32[]{:S(2)}) collective-permute-start(bf16[24,16,128]{2,1,0:T(8,128)(2,1)S(1)} %get-tuple-element.83), channel_id=1, source_target_pairs={{0,2},{1,3},{2,4},{3,5},{4,6},{5,7},{6,0},{7,1},{8,10},{9,11},{10,... | collective-permute-start | bytes 294920 | tf_op jit(solution)/shard_map/ppermute | solution.py:151
  243.5 7.8 %collective-permute-start.30 = (bf16[24,16,128]{2,1,0:T(8,128)(2,1)S(1)}, bf16[24,16,128]{2,1,0:T(8,128)(2,1)S(1)}, u32[]{:S(2)}, u32[]{:S(2)}) collective-permute-start(bf16[24,16,128]{2,1,0:T(8,128)(2,1)S(1)} %get-tuple-element.85), channel_id=1, source_target_pairs={{0,4},{1,5},{2,6},{3,7},{4,0},{5,1},{6,2},{7,3},{8,12},{9,13},{10,... | collective-permute-start | bytes 294920 | tf_op jit(solution)/shard_map/ppermute | solution.py:151
  244.6 6.7 %collective-permute-start.31 = (bf16[24,16,128]{2,1,0:T(8,128)(2,1)S(1)}, bf16[24,16,128]{2,1,0:T(8,128)(2,1)S(1)}, u32[]{:S(2)}, u32[]{:S(2)}) collective-permute-start(bf16[24,16,128]{2,1,0:T(8,128)(2,1)S(1)} %get-tuple-element.84), channel_id=1, source_target_pairs={{0,6},{1,7},{2,0},{3,1},{4,2},{5,3},{6,4},{7,5},{8,14},{9,15},{10,... | collective-permute-start | bytes 294920 | tf_op jit(solution)/shard_map/ppermute | solution.py:151
Sparse Core Ops, SparseCore 0:
  29.1 74.2 all-gather.1
where the time goes:
time: 260 us; the launch traced here: 259 us
  Pallas kernels  105 us (40%)
  waiting for transfers between devices  69.2 us (27%)
  starting transfers between devices  33.5 us (13%)
  local copies, waits for them, and re-layouts  25.2 us (10%)
  between operations  13.6 us (5%)
  other arithmetic  12.5 us (5%)
    ppermute x32, waiting for transfers between devices, shift(): return lax.ppermute(x, ('grp', 'tile'), pairs_of)  69.2 us
    pallas_call x3, Pallas kernels, ladder(): pl.pallas_call(ladder_kernel, grid_spec=pltpu.PrefetchScalarGridSpec(num_...  53.9 us
    pallas_call x3, Pallas kernels, partial_integrals(): pl.pallas_call(integrals_kernel, grid=(c_all // CGROUP,), in_specs=[pl.Bl...  51.2 us
    ppermute x32, starting transfers between devices, shift(): return lax.ppermute(x, ('grp', 'tile'), pairs_of)  33.5 us
    unnamed x16, local copies, waits for them, and re-layouts  14.2 us
    convert_element_type x3, other arithmetic, on_device(): parts.append((halves[0].astype(f32) + halves[1].astype(f32)).astype(bf16))  5.37 us
  transfers between devices with their start and end apart: 33, of which 20 were waited for; matrix products, arithmetic and copies ran while one was open for 8% of the time, Pallas kernels for 20%

commit v1 on v0

--- a/solution.py
+++ b/solution.py
@@ -9,7 +9,7 @@
 VB = 64
 NB = 64
 IJB = 64
-SPLIT = (16, 24, 24)
+SPLIT = (24, 24, 16)
 CGROUP = 4
 ROW_BLOCK = 512
 VMEM_BYTES = 60 * 1024 * 1024
@@ -173,7 +173,12 @@
 
     starts = [sum(SPLIT[:n]) for n in range(len(SPLIT))]
     owns = [window[s : s + size] for s, size in zip(starts, SPLIT)]
-    others = [[shift(own, by_high=k) for k in range(1, high)] for own in owns]
+    others = []
+    for n, own in enumerate(owns):
+        others.append([])
+        for k in range(1, high):
+            others[n].append(shift(own, by_high=k))
+    left, *others[0] = lax.optimization_barrier((left, *others[0]))
     integrals = []
     for n, own in enumerate(owns):
         held = [own] + others[n]

time: 260 us -> 233 us (0.90)
  waiting for transfers between devices: 69.2 us -> 31.9 us
  starting transfers between devices: 33.5 us -> 44.2 us
    ppermute x32, waiting for transfers between devices: 69.2 us -> 31.9 us  [shift(): return lax.ppermute(x, ('grp', 'tile'), pairs_of)]
    ppermute x32, starting transfers between devices: 33.5 us -> 44.2 us  [shift(): return lax.ppermute(x, ('grp', 'tile'), pairs_of)]
  transfers between devices with their start and end apart: 33 -> 33, of which waited for: 20 -> 16; matrix products, arithmetic and copies ran while one was open for 8% -> 9% of each run, Pallas kernels for 20% -> 28%
where the time goes in v1:
time: 233 us; the launch traced here: 232 us
  Pallas kernels  105 us (45%)
  starting transfers between devices  44.2 us (19%)
  waiting for transfers between devices  31.9 us (14%)
  local copies, waits for them, and re-layouts  25.6 us (11%)
  between operations  13.6 us (6%)
  other arithmetic  11.8 us (5%)
    pallas_call x3, Pallas kernels, ladder(): pl.pallas_call(ladder_kernel, grid_spec=pltpu.PrefetchScalarGridSpec(num_...  54 us
    pallas_call x3, Pallas kernels, partial_integrals(): pl.pallas_call(integrals_kernel, grid=(c_all // CGROUP,), in_specs=[pl.Bl...  51.2 us
    ppermute x32, starting transfers between devices, shift(): return lax.ppermute(x, ('grp', 'tile'), pairs_of)  44.2 us
    ppermute x32, waiting for transfers between devices, shift(): return lax.ppermute(x, ('grp', 'tile'), pairs_of)  31.9 us
    unnamed x16, local copies, waits for them, and re-layouts  15.3 us
    convert_element_type x3, other arithmetic, on_device(): parts.append((halves[0].astype(f32) + halves[1].astype(f32)).astype(bf16))  5.59 us
  transfers between devices with their start and end apart: 33, of which 16 were waited for; matrix products, arithmetic and copies ran while one was open for 9% of the time, Pallas kernels for 28%

profile of v1, /device:TPU:0, one launch (start us, length us, event | category | flops | bytes accessed | tf_op | source)
XLA Modules:
  0.0 232.2 jit_solution(5432074166101008836)
XLA Ops:
  6.5 0.9 fusion.30
  7.6 1.1 multiply_bitcast_fusion
  8.6 1.7 copy.8
  10.3 0.8 reshape.96
  11.2 0.6 collective-permute-start
  11.8 1.2 collective-permute-done
  13.0 2.9 %collective-permute-start.1 = (bf16[2,32,2048]{2,1,0:T(8,128)(2,1)S(1)}, bf16[2,32,2048]{2,1,0:T(8,128)(2,1)S(1)}, u32[]{:S(2)}, u32[]{:S(2)}) collective-permute-start(bf16[2,32,2048]{2,1,0:T(8,128)(2,1)S(1)} %get-tuple-element.80), channel_id=1, source_target_pairs={{0,16},{1,17},{2,18},{3,19},{4,20},{5,21},{6,22},{7,23},{8,24},{9,... | collective-permute-start | bytes 786440 | tf_op jit(solution)/shard_map/ppermute | solution.py:151
  15.9 5.8 %copy.13 = bf16[512,32,64]{0,1,2:T(8,128)(2,1)S(1)} copy(bf16[512,32,64]{2,1,0:T(8,128)(2,1)} %bitcast.83) | data formatting | bytes 4194304
  21.7 0.8 collective-permute-done.1
  22.5 0.8 pad_maximum_fusion
  23.3 2.1 reshape.97
  25.4 1.1 copy.9
  26.5 2.4 %copy.10 = bf16[64,4096]{1,0:T(8,128)(2,1)} copy(bf16[64,4096]{0,1:T(8,128)(2,1)} %bitcast.90) | data formatting | bytes 1048576 | tf_op jit(solution)/shard_map/reshape | solution.py:170
  28.9 1.0 fusion.33
  29.9 1.7 collective-permute-start.3
  31.7 7.7 %copy.11 = bf16[512,32,128]{0,2,1:T(8,128)(2,1)} copy(bf16[512,32,128]{2,1,0:T(8,128)(2,1)} %param.3) | data formatting | bytes 8388608 | tf_op args[0]
  39.3 9.9 %collective-permute-done.3.refs_3_ = bf16[24,32,512]{2,1,0:T(8,128)(2,1)} collective-permute-done((bf16[24,32,512]{2,1,0:T(8,128)(2,1)}, bf16[24,32,512]{2,1,0:T(8,128)(2,1)}, u32[]{:S(2)}, u32[]{:S(2)}) %collective-permute-start.3) | collective-permute-done | bytes 786464 | tf_op jit(solution)/shard_map/ppermute | solution.py:151
  49.3 1.5 collective-permute-start.2
  50.7 1.2 collective-permute-done.5.refs_4_
  51.9 18.6 %partial_integrals.3.integrals_ref = bf16[3072,4096]{1,0:T(8,128)(2,1)} custom-call(bf16[4096,512]{1,0:T(8,128)(2,1)} %bitcast.86, bf16[24,32,512]{2,1,0:T(8,128)(2,1)} %get-tuple-element.78.refs_1_, bf16[24,32,512]{2,1,0:T(8,128)(2,1)} %collective-permute-done.4.refs_2_, bf16[24,32,512]{2,1,0:T(8,128)(2,1)} %collective-permute-done.3.refs_3_, ...), custom_call_target="tpu_custom_call" | custom-call | flops 12884901888 | bytes 32505856 | tf_op jit(solution)/shard_map/partial_integrals/pallas_call | solution.py:43
  70.7 0.4 collective-permute-start.8
  71.1 1.5 collective-permute-start.6
  72.9 0.9 copy-done.3
  73.8 0.3 collective-permute-done.8.refs_4_
  74.1 18.6 %partial_integrals.4.integrals_ref = bf16[3072,4096]{1,0:T(8,128)(2,1)} custom-call(bf16[4096,512]{1,0:T(8,128)(2,1)} %bitcast.87, bf16[24,32,512]{2,1,0:T(8,128)(2,1)} %copy-done.1, bf16[24,32,512]{2,1,0:T(8,128)(2,1)} %copy-done.3, bf16[24,32,512]{2,1,0:T(8,128)(2,1)} %collective-permute-done.2.refs_3_, bf16[24,32,512]{2,1,0:T(8,128)(2,1)} %collective-permute-done.8.refs_4_), custom_call_target="tpu_custom_call" | custom-call | flops 12884901888 | bytes 32505856 | tf_op jit(solution)/shard_map/partial_integrals/pallas_call | solution.py:43
  92.9 0.4 collective-permute-start.9
  93.3 0.6 pad_add_fusion.place_ref
  93.9 0.8 collective-permute-done.10.refs_4_
  94.7 0.7 collective-permute-done.9.refs_2_
  95.5 0.8 copy-done.6
  96.3 14.0 %partial_integrals.5.integrals_ref = bf16[2048,4096]{1,0:T(8,128)(2,1)} custom-call(bf16[4096,512]{1,0:T(8,128)(2,1)} %bitcast.88, bf16[16,32,512]{2,1,0:T(8,128)(2,1)} %copy-done.2, bf16[16,32,512]{2,1,0:T(8,128)(2,1)} %copy-done.6, bf16[16,32,512]{2,1,0:T(8,128)(2,1)} %copy-done.4, bf16[16,32,512]{2,1,0:T(8,128)(2,1)} %copy-done.5), custom_call_target="tpu_custom_call" | custom-call | flops 8589934592 | bytes 23068672 | tf_op jit(solution)/shard_map/partial_integrals/pallas_call | solution.py:43
  110.3 19.6 %ladder.3 = (bf16[2,2,4,24,16,128]{5,4,3,2,1,0:T(8,128)(2,1)}, bf16[2,2,4,24,16,128]{5,4,3,2,1,0:T(8,128)(2,1)}) custom-call(s32[3]{0:T(128)} %pad_add_fusion.place_ref, bf16[3072,4096]{1,0:T(8,128)(2,1)} %partial_integrals.3.integrals_ref, bf16[512,4096]{1,0:T(8,128)(2,1)} %all-gather.2.cloned.1.call-done.amps_ref), custom_call_target="tpu_custom_call" | custom-call | flops 12884901888 | bytes 32505856 | tf_op jit(solution)/shard_map/ladder/pallas_call | solution.py:102
  130.1 3.5 %collective-permute-done.11 = bf16[2,2,4,24,16,128]{5,4,3,2,1,0:T(8,128)(2,1)S(1)} collective-permute-done((bf16[2,2,4,24,16,128]{5,4,3,2,1,0:T(8,128)(2,1)}, bf16[2,2,4,24,16,128]{5,4,3,2,1,0:T(8,128)(2,1)S(1)}, u32[]{:S(2)}, u32[]{:S(2)}) %collective-permute-start.11) | collective-permute-done | bytes 1572896 | tf_op jit(solution)/shard_map/ppermute | solution.py:151
  133.6 2.7 %fusion.7 = (bf16[4,24,16,128]{3,2,1,0:T(8,128)(2,1)S(1)}, bf16[4,24,16,128]{3,2,1,0:T(8,128)(2,1)}, bf16[4,24,16,128]{3,2,1,0:T(8,128)(2,1)}, bf16[4,24,16,128]{3,2,1,0:T(8,128)(2,1)S(1)}) fusion(bf16[2,2,4,24,16,128]{5,4,3,2,1,0:T(8,128)(2,1)S(1)} %collective-permute-done.11, bf16[2,2,4,24,16,128]{5,4,3,2,1,0:T(8,128)(2,1)} %get-tuple-element.49), kind=kLoop, calls=%fused_computation.29 | loop fusion | flops 3145728 | bytes 4718592 | tf_op jit(solution)/shard_map/convert_element_type | solution.py:209
  136.2 19.6 %ladder.4 = (bf16[2,2,4,24,16,128]{5,4,3,2,1,0:T(8,128)(2,1)}, bf16[2,2,4,24,16,128]{5,4,3,2,1,0:T(8,128)(2,1)}) custom-call(s32[3]{0:T(128)} %pad_add_fusion.place_ref, bf16[3072,4096]{1,0:T(8,128)(2,1)} %partial_integrals.4.integrals_ref, bf16[512,4096]{1,0:T(8,128)(2,1)} %all-gather.2.cloned.1.call-done.amps_ref), custom_call_target="tpu_custom_call" | custom-call | flops 12884901888 | bytes 32505856 | tf_op jit(solution)/shard_map/ladder/pallas_call | solution.py:102
  156.0 1.5 collective-permute-start.12
  157.5 1.5 collective-permute-start.13
  159.0 0.5 collective-permute-start.14
  159.5 2.7 %fusion.11 = (bf16[4,24,16,128]{3,2,1,0:T(8,128)(2,1)}, bf16[4,24,16,128]{3,2,1,0:T(8,128)(2,1)}, bf16[4,24,16,128]{3,2,1,0:T(8,128)(2,1)}, bf16[4,24,16,128]{3,2,1,0:T(8,128)(2,1)S(1)}) fusion(bf16[2,2,4,24,16,128]{5,4,3,2,1,0:T(8,128)(2,1)S(1)} %collective-permute-done.18, bf16[2,2,4,24,16,128]{5,4,3,2,1,0:T(8,128)(2,1)} %get-tuple-element.57), kind=kLoop, calls=%fused_computation.33 | loop fusion | flops 3145728 | bytes 4718592 | tf_op jit(solution)/shard_map/convert_element_type | solution.py:209
  162.2 14.7 %ladder.5 = (bf16[2,2,4,16,16,128]{5,4,3,2,1,0:T(8,128)(2,1)}, bf16[2,2,4,16,16,128]{5,4,3,2,1,0:T(8,128)(2,1)}) custom-call(s32[3]{0:T(128)} %pad_add_fusion.place_ref, bf16[2048,4096]{1,0:T(8,128)(2,1)} %partial_integrals.5.integrals_ref, bf16[512,4096]{1,0:T(8,128)(2,1)} %all-gather.2.cloned.1.call-done.amps_ref), custom_call_target="tpu_custom_call" | custom-call | flops 8589934592 | bytes 23068672 | tf_op jit(solution)/shard_map/ladder/pallas_call | solution.py:102
  177.3 1.5 add_convert_fusion.5
  178.9 1.6 collective-permute-start.15
  180.5 2.6 %collective-permute-start.16 = (bf16[24,16,128]{2,1,0:T(8,128)(2,1)S(1)}, bf16[24,16,128]{2,1,0:T(8,128)(2,1)S(1)}, u32[]{:S(2)}, u32[]{:S(2)}) collective-permute-start(bf16[24,16,128]{2,1,0:T(8,128)(2,1)S(1)} %get-tuple-element.86), channel_id=1, source_target_pairs={{0,4},{1,5},{2,6},{3,7},{4,0},{5,1},{6,2},{7,3},{8,12},{9,13},{10,... | collective-permute-start | bytes 294920 | tf_op jit(solution)/shard_map/ppermute | solution.py:151
  183.1 1.3 collective-permute-start.17
  184.4 0.8 fusion.32
  185.3 1.5 collective-permute-start.19
  186.8 1.5 collective-permute-start.20
  188.3 1.7 collective-permute-done.16
  190.0 2.4 %collective-permute-start.21 = (bf16[4,24,16,128]{3,2,1,0:T(8,128)(2,1)}, bf16[4,24,16,128]{3,2,1,0:T(8,128)(2,1)S(1)}, u32[]{:S(2)}, u32[]{:S(2)}) collective-permute-start(bf16[4,24,16,128]{3,2,1,0:T(8,128)(2,1)} %get-tuple-element.62), channel_id=1, source_target_pairs={{0,17},{1,16},{2,19},{3,18},{4,21},{5,20},{6,23},{7,22},{8,25},{9,... | collective-permute-start | bytes 1179656 | tf_op jit(solution)/shard_map/ppermute | solution.py:151
  192.7 0.6 collective-permute-start.26
  193.3 0.5 collective-permute-start.27
  193.8 5.0 %collective-permute-done.19 = bf16[4,24,16,128]{3,2,1,0:T(8,128)(2,1)S(1)} collective-permute-done((bf16[4,24,16,128]{3,2,1,0:T(8,128)(2,1)}, bf16[4,24,16,128]{3,2,1,0:T(8,128)(2,1)S(1)}, u32[]{:S(2)}, u32[]{:S(2)}) %collective-permute-start.19) | collective-permute-done | bytes 393248 | tf_op jit(solution)/shard_map/ppermute | solution.py:151
  198.9 8.0 %collective-permute-start.28 = (bf16[4,16,16,128]{3,2,1,0:T(8,128)(2,1)S(1)}, bf16[4,16,16,128]{3,2,1,0:T(8,128)(2,1)S(1)}, u32[]{:S(2)}, u32[]{:S(2)}) collective-permute-start(bf16[4,16,16,128]{3,2,1,0:T(8,128)(2,1)S(1)} %get-tuple-element.76), channel_id=1, source_target_pairs={{0,17},{1,16},{2,19},{3,18},{4,21},{5,20},{6,23},{7,22},{8,25},{9,... | collective-permute-start | bytes 786440 | tf_op jit(solution)/shard_map/ppermute | solution.py:151
  206.9 1.2 collective-permute-done.21
  208.3 3.0 %collective-permute-start.22 = (bf16[24,16,128]{2,1,0:T(8,128)(2,1)S(1)}, bf16[24,16,128]{2,1,0:T(8,128)(2,1)S(1)}, u32[]{:S(2)}, u32[]{:S(2)}) collective-permute-start(bf16[24,16,128]{2,1,0:T(8,128)(2,1)S(1)} %get-tuple-element.87), channel_id=1, source_target_pairs={{0,2},{1,3},{2,4},{3,5},{4,6},{5,7},{6,0},{7,1},{8,10},{9,11},{10,... | collective-permute-start | bytes 294920 | tf_op jit(solution)/shard_map/ppermute | solution.py:151
  211.3 1.1 collective-permute-start.23
  212.4 2.8 %collective-permute-start.24 = (bf16[24,16,128]{2,1,0:T(8,128)(2,1)S(1)}, bf16[24,16,128]{2,1,0:T(8,128)(2,1)S(1)}, u32[]{:S(2)}, u32[]{:S(2)}) collective-permute-start(bf16[24,16,128]{2,1,0:T(8,128)(2,1)S(1)} %get-tuple-element.88), channel_id=1, source_target_pairs={{0,6},{1,7},{2,0},{3,1},{4,2},{5,3},{6,4},{7,5},{8,14},{9,15},{10,... | collective-permute-start | bytes 294920 | tf_op jit(solution)/shard_map/ppermute | solution.py:151
  215.3 1.6 collective-permute-done.28
  217.1 0.8 collective-permute-start.29
  218.0 1.5 collective-permute-start.30
  219.5 1.5 collective-permute-start.31
  221.1 2.3 collective-permute-done.29
  223.4 1.2 collective-permute-done.30
  224.6 0.8 copy.12
  (57 shorter events, 2.7 us)
Async XLA Ops:
  6.5 103.8 %all-gather.2.cloned.1.call-start = ((), (), s32[]{:S(2)}) async-start(), calls=%async_computation | async-start | bytes 4718592 | tf_op jit(solution)/shard_map/all_gather | solution.py:171
  11.2 1.7 collective-permute-start
  13.0 9.5 %collective-permute-start.1 = (bf16[2,32,2048]{2,1,0:T(8,128)(2,1)S(1)}, bf16[2,32,2048]{2,1,0:T(8,128)(2,1)S(1)}, u32[]{:S(2)}, u32[]{:S(2)}) collective-permute-start(bf16[2,32,2048]{2,1,0:T(8,128)(2,1)S(1)} %get-tuple-element.80), channel_id=1, source_target_pairs={{0,16},{1,17},{2,18},{3,19},{4,20},{5,21},{6,22},{7,23},{8,24},{9,... | collective-permute-start | bytes 786440 | tf_op jit(solution)/shard_map/ppermute | solution.py:151
  29.9 40.6 %copy-start.1 = (bf16[24,32,512]{2,1,0:T(8,128)(2,1)}, bf16[24,32,512]{2,1,0:T(8,128)(2,1)S(1)}, u32[]{:S(2)}) copy-start(bf16[24,32,512]{2,1,0:T(8,128)(2,1)S(1)} %get-tuple-element.42.refs_1_) | copy-start | bytes 2359300
  29.9 19.3 %collective-permute-start.3 = (bf16[24,32,512]{2,1,0:T(8,128)(2,1)}, bf16[24,32,512]{2,1,0:T(8,128)(2,1)}, u32[]{:S(2)}, u32[]{:S(2)}) collective-permute-start(bf16[24,32,512]{2,1,0:T(8,128)(2,1)} %get-tuple-element.78.refs_1_), channel_id=1, source_target_pairs={{0,16},{1,17},{2,18},{3,19},{4,20},{5,21},{6,22},{7,23},{8,24},{9,... | collective-permute-start | bytes 2359304 | tf_op jit(solution)/shard_map/ppermute | solution.py:151
  39.3 11.4 %collective-permute-start.4 = (bf16[24,32,512]{2,1,0:T(8,128)(2,1)}, bf16[24,32,512]{2,1,0:T(8,128)(2,1)}, u32[]{:S(2)}, u32[]{:S(2)}) collective-permute-start(bf16[24,32,512]{2,1,0:T(8,128)(2,1)} %get-tuple-element.78.refs_1_), channel_id=1, source_target_pairs={{0,8},{1,9},{2,10},{3,11},{4,12},{5,13},{6,14},{7,15},{8,0},{9,1},... | collective-permute-start | bytes 2359304 | tf_op jit(solution)/shard_map/ppermute | solution.py:151
  49.3 2.6 %collective-permute-start.5 = (bf16[24,32,512]{2,1,0:T(8,128)(2,1)}, bf16[24,32,512]{2,1,0:T(8,128)(2,1)}, u32[]{:S(2)}, u32[]{:S(2)}) collective-permute-start(bf16[24,32,512]{2,1,0:T(8,128)(2,1)} %collective-permute-done.3.refs_3_), channel_id=1, source_target_pairs={{0,8},{1,9},{2,10},{3,11},{4,12},{5,13},{6,14},{7,15},{8,0},{9,1},... | collective-permute-start | bytes 2359304 | tf_op jit(solution)/shard_map/ppermute | solution.py:151
  49.3 21.2 %collective-permute-start.2 = (bf16[24,32,512]{2,1,0:T(8,128)(2,1)S(1)}, bf16[24,32,512]{2,1,0:T(8,128)(2,1)}, u32[]{:S(2)}, u32[]{:S(2)}) collective-permute-start(bf16[24,32,512]{2,1,0:T(8,128)(2,1)S(1)} %get-tuple-element.42.refs_1_), channel_id=1, source_target_pairs={{0,16},{1,17},{2,18},{3,19},{4,20},{5,21},{6,22},{7,23},{8,24},{9,... | collective-permute-start | bytes 2359304 | tf_op jit(solution)/shard_map/ppermute | solution.py:151
  70.5 2.4 %collective-permute-start.7 = (bf16[24,32,512]{2,1,0:T(8,128)(2,1)S(1)}, bf16[24,32,512]{2,1,0:T(8,128)(2,1)S(1)}, u32[]{:S(2)}, u32[]{:S(2)}) collective-permute-start(bf16[24,32,512]{2,1,0:T(8,128)(2,1)S(1)} %get-tuple-element.42.refs_1_), channel_id=1, source_target_pairs={{0,8},{1,9},{2,10},{3,11},{4,12},{5,13},{6,14},{7,15},{8,0},{9,1},... | collective-permute-start | bytes 2359304 | tf_op jit(solution)/shard_map/ppermute | solution.py:151
  70.7 3.4 %collective-permute-start.8 = (bf16[24,32,512]{2,1,0:T(8,128)(2,1)}, bf16[24,32,512]{2,1,0:T(8,128)(2,1)}, u32[]{:S(2)}, u32[]{:S(2)}) collective-permute-start(bf16[24,32,512]{2,1,0:T(8,128)(2,1)} %collective-permute-done.2.refs_3_), channel_id=1, source_target_pairs={{0,8},{1,9},{2,10},{3,11},{4,12},{5,13},{6,14},{7,15},{8,0},{9,1},... | collective-permute-start | bytes 2359304 | tf_op jit(solution)/shard_map/ppermute | solution.py:151
  71.1 21.8 %copy-start.2 = (bf16[16,32,512]{2,1,0:T(8,128)(2,1)}, bf16[16,32,512]{2,1,0:T(8,128)(2,1)S(1)}, u32[]{:S(2)}) copy-start(bf16[16,32,512]{2,1,0:T(8,128)(2,1)S(1)} %slice.90.refs_1_) | copy-start | bytes 1572868
  71.1 21.6 %collective-permute-start.6 = (bf16[16,32,512]{2,1,0:T(8,128)(2,1)S(1)}, bf16[16,32,512]{2,1,0:T(8,128)(2,1)S(1)}, u32[]{:S(2)}, u32[]{:S(2)}) collective-permute-start(bf16[16,32,512]{2,1,0:T(8,128)(2,1)S(1)} %slice.90.refs_1_), channel_id=1, source_target_pairs={{0,16},{1,17},{2,18},{3,19},{4,20},{5,21},{6,22},{7,23},{8,24},{9,... | collective-permute-start | bytes 1572872 | tf_op jit(solution)/shard_map/ppermute | solution.py:151
  72.9 0.9 copy-start.3
  92.7 2.7 %copy-start.4 = (bf16[16,32,512]{2,1,0:T(8,128)(2,1)}, bf16[16,32,512]{2,1,0:T(8,128)(2,1)S(1)}, u32[]{:S(2)}) copy-start(bf16[16,32,512]{2,1,0:T(8,128)(2,1)S(1)} %collective-permute-done.6.refs_3_) | copy-start | bytes 1572868
  92.7 2.0 collective-permute-start.10
  92.9 2.5 %collective-permute-start.9 = (bf16[16,32,512]{2,1,0:T(8,128)(2,1)S(1)}, bf16[16,32,512]{2,1,0:T(8,128)(2,1)S(1)}, u32[]{:S(2)}, u32[]{:S(2)}) collective-permute-start(bf16[16,32,512]{2,1,0:T(8,128)(2,1)S(1)} %slice.90.refs_1_), channel_id=1, source_target_pairs={{0,8},{1,9},{2,10},{3,11},{4,12},{5,13},{6,14},{7,15},{8,0},{9,1},... | collective-permute-start | bytes 1572872 | tf_op jit(solution)/shard_map/ppermute | solution.py:151
  94.7 0.8 copy-start.5
  95.5 0.8 copy-start.6
  129.9 3.6 %collective-permute-start.11 = (bf16[2,2,4,24,16,128]{5,4,3,2,1,0:T(8,128)(2,1)}, bf16[2,2,4,24,16,128]{5,4,3,2,1,0:T(8,128)(2,1)S(1)}, u32[]{:S(2)}, u32[]{:S(2)}) collective-permute-start(bf16[2,2,4,24,16,128]{5,4,3,2,1,0:T(8,128)(2,1)} %get-tuple-element.50), channel_id=1, source_target_pairs={{0,8},{1,9},{2,10},{3,11},{4,12},{5,13},{6,14},{7,15},{8,0},{9,1},... | collective-permute-start | bytes 4718600 | tf_op jit(solution)/shard_map/ppermute | solution.py:151
  155.9 3.6 %collective-permute-start.18 = (bf16[2,2,4,24,16,128]{5,4,3,2,1,0:T(8,128)(2,1)}, bf16[2,2,4,24,16,128]{5,4,3,2,1,0:T(8,128)(2,1)S(1)}, u32[]{:S(2)}, u32[]{:S(2)}) collective-permute-start(bf16[2,2,4,24,16,128]{5,4,3,2,1,0:T(8,128)(2,1)} %get-tuple-element.58), channel_id=1, source_target_pairs={{0,8},{1,9},{2,10},{3,11},{4,12},{5,13},{6,14},{7,15},{8,0},{9,1},... | collective-permute-start | bytes 4718600 | tf_op jit(solution)/shard_map/ppermute | solution.py:151
  156.0 21.0 %collective-permute-start.12 = (bf16[4,24,16,128]{3,2,1,0:T(8,128)(2,1)}, bf16[4,24,16,128]{3,2,1,0:T(8,128)(2,1)}, u32[]{:S(2)}, u32[]{:S(2)}) collective-permute-start(bf16[4,24,16,128]{3,2,1,0:T(8,128)(2,1)} %get-tuple-element.52), channel_id=1, source_target_pairs={{0,1},{1,0},{2,3},{3,2},{4,5},{5,4},{6,7},{7,6},{8,9},{9,8},{10,11... | collective-permute-start | bytes 1179656 | tf_op jit(solution)/shard_map/ppermute | solution.py:151
  157.5 19.5 %collective-permute-start.13 = (bf16[4,24,16,128]{3,2,1,0:T(8,128)(2,1)}, bf16[4,24,16,128]{3,2,1,0:T(8,128)(2,1)}, u32[]{:S(2)}, u32[]{:S(2)}) collective-permute-start(bf16[4,24,16,128]{3,2,1,0:T(8,128)(2,1)} %get-tuple-element.53), channel_id=1, source_target_pairs={{0,16},{1,17},{2,18},{3,19},{4,20},{5,21},{6,22},{7,23},{8,24},{9,... | collective-permute-start | bytes 1179656 | tf_op jit(solution)/shard_map/ppermute | solution.py:151
  159.0 18.3 %collective-permute-start.14 = (bf16[4,24,16,128]{3,2,1,0:T(8,128)(2,1)S(1)}, bf16[4,24,16,128]{3,2,1,0:T(8,128)(2,1)}, u32[]{:S(2)}, u32[]{:S(2)}) collective-permute-start(bf16[4,24,16,128]{3,2,1,0:T(8,128)(2,1)S(1)} %get-tuple-element.54), channel_id=1, source_target_pairs={{0,17},{1,16},{2,19},{3,18},{4,21},{5,20},{6,23},{7,22},{8,25},{9,... | collective-permute-start | bytes 1179656 | tf_op jit(solution)/shard_map/ppermute | solution.py:151
  176.9 15.6 %collective-permute-start.25 = (bf16[2,2,4,16,16,128]{5,4,3,2,1,0:T(8,128)(2,1)}, bf16[2,2,4,16,16,128]{5,4,3,2,1,0:T(8,128)(2,1)S(1)}, u32[]{:S(2)}, u32[]{:S(2)}) collective-permute-start(bf16[2,2,4,16,16,128]{5,4,3,2,1,0:T(8,128)(2,1)} %get-tuple-element.66), channel_id=1, source_target_pairs={{0,8},{1,9},{2,10},{3,11},{4,12},{5,13},{6,14},{7,15},{8,0},{9,1},... | collective-permute-start | bytes 3145736 | tf_op jit(solution)/shard_map/ppermute | solution.py:151
  177.1 15.4 %copy-start = (bf16[2,2,4,16,16,128]{5,4,3,2,1,0:T(8,128)(2,1)S(1)}, bf16[2,2,4,16,16,128]{5,4,3,2,1,0:T(8,128)(2,1)}, u32[]{:S(2)}) copy-start(bf16[2,2,4,16,16,128]{5,4,3,2,1,0:T(8,128)(2,1)} %get-tuple-element.65) | copy-start | bytes 3145732
  178.9 8.0 %collective-permute-start.15 = (bf16[24,16,128]{2,1,0:T(8,128)(2,1)S(1)}, bf16[24,16,128]{2,1,0:T(8,128)(2,1)S(1)}, u32[]{:S(2)}, u32[]{:S(2)}) collective-permute-start(bf16[24,16,128]{2,1,0:T(8,128)(2,1)S(1)} %get-tuple-element.84), channel_id=1, source_target_pairs={{0,2},{1,3},{2,4},{3,5},{4,6},{5,7},{6,0},{7,1},{8,10},{9,11},{10,... | collective-permute-start | bytes 294920 | tf_op jit(solution)/shard_map/ppermute | solution.py:151
  180.5 9.5 %collective-permute-start.16 = (bf16[24,16,128]{2,1,0:T(8,128)(2,1)S(1)}, bf16[24,16,128]{2,1,0:T(8,128)(2,1)S(1)}, u32[]{:S(2)}, u32[]{:S(2)}) collective-permute-start(bf16[24,16,128]{2,1,0:T(8,128)(2,1)S(1)} %get-tuple-element.86), channel_id=1, source_target_pairs={{0,4},{1,5},{2,6},{3,7},{4,0},{5,1},{6,2},{7,3},{8,12},{9,13},{10,... | collective-permute-start | bytes 294920 | tf_op jit(solution)/shard_map/ppermute | solution.py:151
  183.1 9.4 %collective-permute-start.17 = (bf16[24,16,128]{2,1,0:T(8,128)(2,1)S(1)}, bf16[24,16,128]{2,1,0:T(8,128)(2,1)S(1)}, u32[]{:S(2)}, u32[]{:S(2)}) collective-permute-start(bf16[24,16,128]{2,1,0:T(8,128)(2,1)S(1)} %get-tuple-element.85), channel_id=1, source_target_pairs={{0,6},{1,7},{2,0},{3,1},{4,2},{5,3},{6,4},{7,5},{8,14},{9,15},{10,... | collective-permute-start | bytes 294920 | tf_op jit(solution)/shard_map/ppermute | solution.py:151
  185.3 13.5 %collective-permute-start.19 = (bf16[4,24,16,128]{3,2,1,0:T(8,128)(2,1)}, bf16[4,24,16,128]{3,2,1,0:T(8,128)(2,1)S(1)}, u32[]{:S(2)}, u32[]{:S(2)}) collective-permute-start(bf16[4,24,16,128]{3,2,1,0:T(8,128)(2,1)} %get-tuple-element.60), channel_id=1, source_target_pairs={{0,1},{1,0},{2,3},{3,2},{4,5},{5,4},{6,7},{7,6},{8,9},{9,8},{10,11... | collective-permute-start | bytes 1179656 | tf_op jit(solution)/shard_map/ppermute | solution.py:151
  186.8 20.0 %collective-permute-start.20 = (bf16[4,24,16,128]{3,2,1,0:T(8,128)(2,1)}, bf16[4,24,16,128]{3,2,1,0:T(8,128)(2,1)S(1)}, u32[]{:S(2)}, u32[]{:S(2)}) collective-permute-start(bf16[4,24,16,128]{3,2,1,0:T(8,128)(2,1)} %get-tuple-element.61), channel_id=1, source_target_pairs={{0,16},{1,17},{2,18},{3,19},{4,20},{5,21},{6,22},{7,23},{8,24},{9,... | collective-permute-start | bytes 1179656 | tf_op jit(solution)/shard_map/ppermute | solution.py:151
  190.0 18.1 %collective-permute-start.21 = (bf16[4,24,16,128]{3,2,1,0:T(8,128)(2,1)}, bf16[4,24,16,128]{3,2,1,0:T(8,128)(2,1)S(1)}, u32[]{:S(2)}, u32[]{:S(2)}) collective-permute-start(bf16[4,24,16,128]{3,2,1,0:T(8,128)(2,1)} %get-tuple-element.62), channel_id=1, source_target_pairs={{0,17},{1,16},{2,19},{3,18},{4,21},{5,20},{6,23},{7,22},{8,25},{9,... | collective-permute-start | bytes 1179656 | tf_op jit(solution)/shard_map/ppermute | solution.py:151
  192.7 19.7 %collective-permute-start.26 = (bf16[4,16,16,128]{3,2,1,0:T(8,128)(2,1)S(1)}, bf16[4,16,16,128]{3,2,1,0:T(8,128)(2,1)S(1)}, u32[]{:S(2)}, u32[]{:S(2)}) collective-permute-start(bf16[4,16,16,128]{3,2,1,0:T(8,128)(2,1)S(1)} %get-tuple-element.75), channel_id=1, source_target_pairs={{0,1},{1,0},{2,3},{3,2},{4,5},{5,4},{6,7},{7,6},{8,9},{9,8},{10,11... | collective-permute-start | bytes 786440 | tf_op jit(solution)/shard_map/ppermute | solution.py:151
  193.3 22.0 %collective-permute-start.27 = (bf16[4,16,16,128]{3,2,1,0:T(8,128)(2,1)S(1)}, bf16[4,16,16,128]{3,2,1,0:T(8,128)(2,1)S(1)}, u32[]{:S(2)}, u32[]{:S(2)}) collective-permute-start(bf16[4,16,16,128]{3,2,1,0:T(8,128)(2,1)S(1)} %get-tuple-element.77), channel_id=1, source_target_pairs={{0,16},{1,17},{2,18},{3,19},{4,20},{5,21},{6,22},{7,23},{8,24},{9,... | collective-permute-start | bytes 786440 | tf_op jit(solution)/shard_map/ppermute | solution.py:151
  198.9 18.0 %collective-permute-start.28 = (bf16[4,16,16,128]{3,2,1,0:T(8,128)(2,1)S(1)}, bf16[4,16,16,128]{3,2,1,0:T(8,128)(2,1)S(1)}, u32[]{:S(2)}, u32[]{:S(2)}) collective-permute-start(bf16[4,16,16,128]{3,2,1,0:T(8,128)(2,1)S(1)} %get-tuple-element.76), channel_id=1, source_target_pairs={{0,17},{1,16},{2,19},{3,18},{4,21},{5,20},{6,23},{7,22},{8,25},{9,... | collective-permute-start | bytes 786440 | tf_op jit(solution)/shard_map/ppermute | solution.py:151
  208.3 11.2 %collective-permute-start.22 = (bf16[24,16,128]{2,1,0:T(8,128)(2,1)S(1)}, bf16[24,16,128]{2,1,0:T(8,128)(2,1)S(1)}, u32[]{:S(2)}, u32[]{:S(2)}) collective-permute-start(bf16[24,16,128]{2,1,0:T(8,128)(2,1)S(1)} %get-tuple-element.87), channel_id=1, source_target_pairs={{0,2},{1,3},{2,4},{3,5},{4,6},{5,7},{6,0},{7,1},{8,10},{9,11},{10,... | collective-permute-start | bytes 294920 | tf_op jit(solution)/shard_map/ppermute | solution.py:151
  211.3 9.7 %collective-permute-start.23 = (bf16[24,16,128]{2,1,0:T(8,128)(2,1)S(1)}, bf16[24,16,128]{2,1,0:T(8,128)(2,1)S(1)}, u32[]{:S(2)}, u32[]{:S(2)}) collective-permute-start(bf16[24,16,128]{2,1,0:T(8,128)(2,1)S(1)} %get-tuple-element.89), channel_id=1, source_target_pairs={{0,4},{1,5},{2,6},{3,7},{4,0},{5,1},{6,2},{7,3},{8,12},{9,13},{10,... | collective-permute-start | bytes 294920 | tf_op jit(solution)/shard_map/ppermute | solution.py:151
  212.4 8.6 %collective-permute-start.24 = (bf16[24,16,128]{2,1,0:T(8,128)(2,1)S(1)}, bf16[24,16,128]{2,1,0:T(8,128)(2,1)S(1)}, u32[]{:S(2)}, u32[]{:S(2)}) collective-permute-start(bf16[24,16,128]{2,1,0:T(8,128)(2,1)S(1)} %get-tuple-element.88), channel_id=1, source_target_pairs={{0,6},{1,7},{2,0},{3,1},{4,2},{5,3},{6,4},{7,5},{8,14},{9,15},{10,... | collective-permute-start | bytes 294920 | tf_op jit(solution)/shard_map/ppermute | solution.py:151
  217.1 6.2 %collective-permute-start.29 = (bf16[16,16,128]{2,1,0:T(8,128)(2,1)S(1)}, bf16[16,16,128]{2,1,0:T(8,128)(2,1)S(1)}, u32[]{:S(2)}, u32[]{:S(2)}) collective-permute-start(bf16[16,16,128]{2,1,0:T(8,128)(2,1)S(1)} %get-tuple-element.90), channel_id=1, source_target_pairs={{0,2},{1,3},{2,4},{3,5},{4,6},{5,7},{6,0},{7,1},{8,10},{9,11},{10,... | collective-permute-start | bytes 196616 | tf_op jit(solution)/shard_map/ppermute | solution.py:151
  218.0 6.6 %collective-permute-start.30 = (bf16[16,16,128]{2,1,0:T(8,128)(2,1)S(1)}, bf16[16,16,128]{2,1,0:T(8,128)(2,1)S(1)}, u32[]{:S(2)}, u32[]{:S(2)}) collective-permute-start(bf16[16,16,128]{2,1,0:T(8,128)(2,1)S(1)} %get-tuple-element.92), channel_id=1, source_target_pairs={{0,4},{1,5},{2,6},{3,7},{4,0},{5,1},{6,2},{7,3},{8,12},{9,13},{10,... | collective-permute-start | bytes 196616 | tf_op jit(solution)/shard_map/ppermute | solution.py:151
  219.5 5.0 %collective-permute-start.31 = (bf16[16,16,128]{2,1,0:T(8,128)(2,1)S(1)}, bf16[16,16,128]{2,1,0:T(8,128)(2,1)S(1)}, u32[]{:S(2)}, u32[]{:S(2)}) collective-permute-start(bf16[16,16,128]{2,1,0:T(8,128)(2,1)S(1)} %get-tuple-element.91), channel_id=1, source_target_pairs={{0,6},{1,7},{2,0},{3,1},{4,2},{5,3},{6,4},{7,5},{8,14},{9,15},{10,... | collective-permute-start | bytes 196616 | tf_op jit(solution)/shard_map/ppermute | solution.py:151
Sparse Core Ops, SparseCore 0:
  29.0 74.2 all-gather.1

commit v2 on v1

--- a/solution.py
+++ b/solution.py
@@ -56,10 +56,10 @@
     )(left, *pieces)
 
 
-def ladder_kernel(place_ref, integrals_ref, amps_ref, keep_ref, send_ref):
-    high, quarter = keep_ref.shape[0], keep_ref.shape[-1]
+def ladder_kernel(place_ref, mask_ref, integrals_ref, amps_ref, keep_ref, send_ref):
+    high, _, quarter = keep_ref.shape
     low = 2
-    core, chip_x, near = place_ref[0], place_ref[1], place_ref[2]
+    core, chip_x = place_ref[0], place_ref[1]
     half = lax.dot_general(
         integrals_ref[...], amps_ref[...], (((1,), (1,)), ((), ())), preferred_element_type=jnp.float32
     ).astype(jnp.bfloat16)
@@ -68,47 +68,115 @@
         blocks = [
             half[:, (h * low + c) * quarter : (h * low + c + 1) * quarter] for c in range(low)
         ]
-        keep = jnp.where(core == 0, blocks[0], blocks[1])
-        send = jnp.where(core == 0, blocks[1], blocks[0])
-        if len(keep_ref.shape) == 3:
-            keep_ref[slot], send_ref[slot] = keep, send
-            continue
-        _, inner, outer, bs, a_local, _ = keep_ref.shape
-        a_all = outer * inner * a_local
-        for i in range(inner):
-            at = lax.rem(i - near + inner, inner)
-            for b in range(bs):
-                for o in range(outer):
-                    row = b * a_all + (o * inner + i) * a_local
-                    keep_ref[slot, at, o, b] = keep[row : row + a_local]
-                    send_ref[slot, at, o, b] = send[row : row + a_local]
-
-
-def ladder(place, integrals, amps, high, low, split):
+        keep_ref[slot] = jnp.where(core == 0, blocks[0], blocks[1])
+        send_ref[slot] = jnp.where(core == 0, blocks[1], blocks[0])
+
+
+def tiled_ladder_kernel(
+    place_ref, mask_ref, integrals_ref, amps_ref, keep_ref, send_ref, list_ref, full_ref
+):
+    high, inner, outer, bs, a_local, quarter = keep_ref.shape
+    low = 2
+    _, _, a_block, depth = integrals_ref.shape
+    slots, few = list_ref.shape[0], list_ref.shape[0] // 2
+    v_blocks = mask_ref.shape[0] // slots
+    wide = round(v_blocks**0.5)
+    core, chip_x, near, c_block = (place_ref[i] for i in range(4))
+    a_at = pl.program_id(1)
+
+    listed = jnp.int32(0)
+    for n in range(slots):
+        shown = mask_ref[n * v_blocks + a_at * wide] != 0
+        kept = mask_ref[n * v_blocks + c_block * wide] != 0
+        for d in range(1, wide):
+            kept = jnp.logical_or(kept, mask_ref[n * v_blocks + c_block * wide + d] != 0)
+        active = jnp.logical_and(shown, kept)
+        list_ref[jnp.where(active, listed, slots - 1 - n + listed)] = jnp.int32(n)
+        listed = listed + active.astype(jnp.int32)
+
+    def product(amps):
+        rows = integrals_ref[...].reshape(bs * a_block, depth)
+        return lax.dot_general(
+            rows, amps, (((1,), (1,)), ((), ())), preferred_element_type=jnp.float32
+        ).astype(jnp.bfloat16)
+
+    def emit(quarters):
+        for h in range(high):
+            slot = lax.rem(h - chip_x + high, high)
+            first, second = quarters[h * low], quarters[h * low + 1]
+            keep = jnp.where(core == 0, first, second)
+            send = jnp.where(core == 0, second, first)
+            for i in range(inner):
+                at = lax.rem(i - near + inner, inner)
+                for b in range(bs):
+                    for o in range(outer):
+                        row = b * a_block + (o * inner + i) * a_local
+                        keep_ref[slot, at, o, b] = keep[row : row + a_local]
+                        send_ref[slot, at, o, b] = send[row : row + a_local]
+
+    @pl.when(listed <= few)
+    def _():
+        full_ref[...] = jnp.zeros_like(full_ref)
+        at = [list_ref[n] for n in range(few)]
+        some = product(
+            jnp.concatenate(
+                [amps_ref[pl.ds(pl.multiple_of(n * IJB, IJB), IJB), :] for n in at], axis=0
+            )
+        )
+        per = quarter // IJB
+        for n, index in enumerate(at):
+            for k in range(per):
+
+                @pl.when(lax.rem(index, per) == k)
+                def _():
+                    full_ref[lax.div(index, per), :, k * IJB : (k + 1) * IJB] = some[
+                        :, n * IJB : (n + 1) * IJB
+                    ]
+
+        emit([full_ref[q] for q in range(high * low)])
+
+    @pl.when(listed > few)
+    def _():
+        every = product(amps_ref[...])
+        emit([every[:, q * quarter : (q + 1) * quarter] for q in range(high * low)])
+
+
+def ladder(place, mask, integrals, amps, high, low, split):
     rows, inner = integrals.shape
     pairs = amps.shape[0]
     quarter = pairs // (high * low)
-    block = ROW_BLOCK * 512 // max(512, pairs)
-    if split[-1] % 16:
-        shape, piece = (high, rows, quarter), (high, block, quarter)
-        spec = pl.BlockSpec(piece, lambda i, place: (0, i, 0))
+    near, far, a_local = split
+    a_all = near * far * a_local
+    amps_spec = pl.BlockSpec(
+        (pairs, inner), lambda i, j, *_: (0, 0), pipeline_mode=pl.Buffered(1)
+    )
+    if a_local % 16 or quarter % 128 or VB % (near * a_local):
+        block = ROW_BLOCK * 512 // max(512, pairs)
+        kernel, grid, scratch = ladder_kernel, (rows // block, 1), []
+        left_spec = pl.BlockSpec((block, inner), lambda i, j, *_: (i, 0))
+        shape = (high, rows, quarter)
+        spec = pl.BlockSpec((high, block, quarter), lambda i, j, *_: (0, i, 0))
     else:
-        near, far, a_local = split
-        a_all = near * far * a_local
+        bs, parts = ROW_BLOCK // VB, a_all // VB
+        kernel, grid = tiled_ladder_kernel, (rows // a_all // bs, parts)
+        integrals = integrals.reshape(rows // a_all, parts, VB, inner)
+        left_spec = pl.BlockSpec((bs, 1, VB, inner), lambda i, j, *_: (i, j, 0, 0))
         shape = (high, near, far, rows // a_all, a_local, quarter)
-        piece = (high, near, far, block // a_all, a_local, quarter)
-        spec = pl.BlockSpec(piece, lambda i, place: (0, 0, 0, i, 0, 0))
+        piece = (high, near, far // parts, bs, a_local, quarter)
+        spec = pl.BlockSpec(piece, lambda i, j, *_: (0, 0, j, i, 0, 0))
+        scratch = [
+            pltpu.SMEM((pairs // IJB,), jnp.int32),
+            pltpu.VMEM((high * low, bs * VB, quarter), jnp.bfloat16),
+        ]
     shape = jax.ShapeDtypeStruct(shape, jnp.bfloat16)
     return pl.pallas_call(
-        ladder_kernel,
+        kernel,
         grid_spec=pltpu.PrefetchScalarGridSpec(
-            num_scalar_prefetch=1,
-            grid=(rows // block,),
-            in_specs=[
-                pl.BlockSpec((block, inner), lambda i, place: (i, 0)),
-                pl.BlockSpec((pairs, inner), lambda i, place: (0, 0), pipeline_mode=pl.Buffered(1)),
-            ],
+            num_scalar_prefetch=2,
+            grid=grid,
+            in_specs=[left_spec, amps_spec],
             out_specs=[spec, spec],
+            scratch_shapes=scratch,
         ),
         out_shape=[shape, shape],
         cost_estimate=pl.CostEstimate(
@@ -118,7 +186,7 @@
         ),
         compiler_params=pltpu.CompilerParams(vmem_limit_bytes=VMEM_BYTES),
         name="ladder",
-    )(place, integrals, amps)
+    )(place, mask, integrals, amps)
 
 
 def pick(x, index, axis):
@@ -190,10 +258,11 @@
         integrals.append(partial_integrals(left, pieces, quarter))
     amps, *integrals = lax.optimization_barrier((amps, *integrals))
 
-    place = jnp.stack([core, chip_x, near]).astype(jnp.int32)
+    place = jnp.stack([core, chip_x, near, grp * quarter // VB]).astype(jnp.int32)
+    mask = tile_mask.reshape(-1)
     chunks = []
     for n, size in enumerate(SPLIT):
-        keep, send = ladder(place, integrals[n], amps, high, low, (inner, outer, a_local))
+        keep, send = ladder(place, mask, integrals[n], amps, high, low, (inner, outer, a_local))
         got = shift(send, by_low=1)
         parts = []
         for kx in range(high):

time: 233 us -> 227 us (0.974)
  Pallas kernels: 105 us -> 96.9 us
  waiting for transfers between devices: 31.9 us -> 34.9 us
    pallas_call x3, Pallas kernels: 54 us -> 45.6 us  [ladder(): pl.pallas_call(kernel, grid_spec=pltpu.PrefetchScalarGridSpec(num_scalar_...]
    ppermute x32, waiting for transfers between devices: 31.9 us -> 34.9 us  [shift(): return lax.ppermute(x, ('grp', 'tile'), pairs_of)]
    unnamed x16 -> x19, local copies, waits for them, and re-layouts: 15.3 us -> 15.4 us
  transfers between devices with their start and end apart: 33 -> 33, of which waited for: 16 -> 17; matrix products, arithmetic and copies ran while one was open for 9% -> 9% of each run, Pallas kernels for 28% -> 28%
where the time goes in v2:
time: 227 us; the launch traced here: 226 us
  Pallas kernels  96.9 us (43%)
  starting transfers between devices  43.1 us (19%)
  waiting for transfers between devices  34.9 us (15%)
  local copies, waits for them, and re-layouts  26.4 us (12%)
  between operations  13.6 us (6%)
  other arithmetic  11.2 us (5%)
    pallas_call x3, Pallas kernels, partial_integrals(): pl.pallas_call(integrals_kernel, grid=(c_all // CGROUP,), in_specs=[pl.Bl...  51.3 us
    pallas_call x3, Pallas kernels, ladder(): pl.pallas_call(kernel, grid_spec=pltpu.PrefetchScalarGridSpec(num_scalar_...  45.6 us
    ppermute x32, starting transfers between devices, shift(): return lax.ppermute(x, ('grp', 'tile'), pairs_of)  43.1 us
    ppermute x32, waiting for transfers between devices, shift(): return lax.ppermute(x, ('grp', 'tile'), pairs_of)  34.9 us
    unnamed x19, local copies, waits for them, and re-layouts  15.4 us
    convert_element_type x3, other arithmetic, on_device(): parts.append((halves[0].astype(f32) + halves[1].astype(f32)).astype(bf16))  5.61 us
  transfers between devices with their start and end apart: 33, of which 17 were waited for; matrix products, arithmetic and copies ran while one was open for 9% of the time, Pallas kernels for 28%

profile of v2, /device:TPU:0, one launch (start us, length us, event | category | flops | bytes accessed | tf_op | source)
XLA Modules:
  0.0 226.1 jit_solution(15809204985317348302)
XLA Ops:
  6.5 0.9 fusion.30
  7.6 1.1 multiply_bitcast_fusion
  8.6 1.7 copy.9
  10.3 0.8 reshape.108
  11.2 0.6 collective-permute-start
  11.8 1.2 collective-permute-done
  13.0 2.9 %collective-permute-start.1 = (bf16[2,32,2048]{2,1,0:T(8,128)(2,1)S(1)}, bf16[2,32,2048]{2,1,0:T(8,128)(2,1)S(1)}, u32[]{:S(2)}, u32[]{:S(2)}) collective-permute-start(bf16[2,32,2048]{2,1,0:T(8,128)(2,1)S(1)} %get-tuple-element.80), channel_id=1, source_target_pairs={{0,16},{1,17},{2,18},{3,19},{4,20},{5,21},{6,22},{7,23},{8,24},{9,... | collective-permute-start | bytes 786440 | tf_op jit(solution)/shard_map/ppermute | solution.py:219
  15.9 5.8 %copy.15 = bf16[512,32,64]{0,1,2:T(8,128)(2,1)S(1)} copy(bf16[512,32,64]{2,1,0:T(8,128)(2,1)} %bitcast.87) | data formatting | bytes 4194304
  21.7 0.8 collective-permute-done.1
  22.5 0.8 pad_maximum_fusion
  23.3 2.1 reshape.109
  25.4 1.1 copy.10
  26.6 2.4 %copy.11 = bf16[64,4096]{1,0:T(8,128)(2,1)} copy(bf16[64,4096]{0,1:T(8,128)(2,1)} %bitcast.94) | data formatting | bytes 1048576 | tf_op jit(solution)/shard_map/reshape | solution.py:238
  28.9 1.0 fusion.33
  30.0 1.7 collective-permute-start.3
  31.7 7.6 %copy.12 = bf16[512,32,128]{0,2,1:T(8,128)(2,1)} copy(bf16[512,32,128]{2,1,0:T(8,128)(2,1)} %param.3) | data formatting | bytes 8388608 | tf_op args[0]
  39.4 9.9 %collective-permute-done.3.refs_3_ = bf16[24,32,512]{2,1,0:T(8,128)(2,1)} collective-permute-done((bf16[24,32,512]{2,1,0:T(8,128)(2,1)}, bf16[24,32,512]{2,1,0:T(8,128)(2,1)}, u32[]{:S(2)}, u32[]{:S(2)}) %collective-permute-start.3) | collective-permute-done | bytes 786464 | tf_op jit(solution)/shard_map/ppermute | solution.py:219
  49.3 1.5 collective-permute-start.2
  50.8 1.2 collective-permute-done.5.refs_4_
  51.9 18.6 %partial_integrals.3 = bf16[3072,4096]{1,0:T(8,128)(2,1)} custom-call(bf16[4096,512]{1,0:T(8,128)(2,1)} %bitcast.90, bf16[24,32,512]{2,1,0:T(8,128)(2,1)} %get-tuple-element.78.refs_1_, bf16[24,32,512]{2,1,0:T(8,128)(2,1)} %collective-permute-done.4.refs_2_, bf16[24,32,512]{2,1,0:T(8,128)(2,1)} %collective-permute-done.3.refs_3_, ...), custom_call_target="tpu_custom_call" | custom-call | flops 12884901888 | bytes 32505856 | tf_op jit(solution)/shard_map/partial_integrals/pallas_call | solution.py:43
  70.8 0.4 collective-permute-start.8
  71.2 1.5 collective-permute-start.6
  72.9 0.9 copy-done.4
  73.8 0.3 collective-permute-done.8.refs_4_
  74.2 18.6 %partial_integrals.4 = bf16[3072,4096]{1,0:T(8,128)(2,1)} custom-call(bf16[4096,512]{1,0:T(8,128)(2,1)} %bitcast.91, bf16[24,32,512]{2,1,0:T(8,128)(2,1)} %copy-done.1, bf16[24,32,512]{2,1,0:T(8,128)(2,1)} %copy-done.4, bf16[24,32,512]{2,1,0:T(8,128)(2,1)} %collective-permute-done.2.refs_3_, bf16[24,32,512]{2,1,0:T(8,128)(2,1)} %collective-permute-done.8.refs_4_), custom_call_target="tpu_custom_call" | custom-call | flops 12884901888 | bytes 32505856 | tf_op jit(solution)/shard_map/partial_integrals/pallas_call | solution.py:43
  93.0 0.4 collective-permute-start.9
  93.5 0.6 reshape.112.mask_ref
  94.1 0.7 pad_add_fusion.place_ref
  94.8 0.7 collective-permute-done.9.refs_2_
  95.6 0.8 copy-done.7
  96.4 14.0 %partial_integrals.5 = bf16[2048,4096]{1,0:T(8,128)(2,1)} custom-call(bf16[4096,512]{1,0:T(8,128)(2,1)} %bitcast.92, bf16[16,32,512]{2,1,0:T(8,128)(2,1)} %copy-done.2, bf16[16,32,512]{2,1,0:T(8,128)(2,1)} %copy-done.7, bf16[16,32,512]{2,1,0:T(8,128)(2,1)} %copy-done.5, bf16[16,32,512]{2,1,0:T(8,128)(2,1)} %copy-done.6), custom_call_target="tpu_custom_call" | custom-call | flops 8589934592 | bytes 23068672 | tf_op jit(solution)/shard_map/partial_integrals/pallas_call | solution.py:43
  110.4 16.5 %ladder.3 = (bf16[2,2,4,24,16,128]{5,4,3,2,1,0:T(8,128)(2,1)}, bf16[2,2,4,24,16,128]{5,4,3,2,1,0:T(8,128)(2,1)}) custom-call(s32[4]{0:T(128)} %pad_add_fusion.place_ref, s32[32]{0:T(128)} %reshape.112.mask_ref, bf16[24,2,64,4096]{3,2,1,0:T(8,128)(2,1)} %bitcast.96, bf16[512,4096]{1,0:T(8,128)(2,1)} %all-gather.2.cloned.1.call-done.amps_ref), custom_call_target="tpu_custom_call" | custom-call | flops 12884901888 | bytes 32505856 | tf_op jit(solution)/shard_map/ladder/pallas_call | solution.py:172
  127.0 3.5 %collective-permute-done.11 = bf16[2,2,4,24,16,128]{5,4,3,2,1,0:T(8,128)(2,1)S(1)} collective-permute-done((bf16[2,2,4,24,16,128]{5,4,3,2,1,0:T(8,128)(2,1)}, bf16[2,2,4,24,16,128]{5,4,3,2,1,0:T(8,128)(2,1)S(1)}, u32[]{:S(2)}, u32[]{:S(2)}) %collective-permute-start.11) | collective-permute-done | bytes 1572896 | tf_op jit(solution)/shard_map/ppermute | solution.py:219
  130.5 2.7 %fusion.7 = (bf16[4,24,16,128]{3,2,1,0:T(8,128)(2,1)S(1)}, bf16[4,24,16,128]{3,2,1,0:T(8,128)(2,1)}, bf16[4,24,16,128]{3,2,1,0:T(8,128)(2,1)}, bf16[4,24,16,128]{3,2,1,0:T(8,128)(2,1)S(1)}) fusion(bf16[2,2,4,24,16,128]{5,4,3,2,1,0:T(8,128)(2,1)S(1)} %collective-permute-done.11, bf16[2,2,4,24,16,128]{5,4,3,2,1,0:T(8,128)(2,1)} %get-tuple-element.49), kind=kLoop, calls=%fused_computation.29 | loop fusion | flops 3145728 | bytes 4718592 | tf_op jit(solution)/shard_map/convert_element_type | solution.py:278
  133.2 16.7 %ladder.4 = (bf16[2,2,4,24,16,128]{5,4,3,2,1,0:T(8,128)(2,1)}, bf16[2,2,4,24,16,128]{5,4,3,2,1,0:T(8,128)(2,1)}) custom-call(s32[4]{0:T(128)} %pad_add_fusion.place_ref, s32[32]{0:T(128)} %reshape.112.mask_ref, bf16[24,2,64,4096]{3,2,1,0:T(8,128)(2,1)} %bitcast.97, bf16[512,4096]{1,0:T(8,128)(2,1)} %all-gather.2.cloned.1.call-done.amps_ref), custom_call_target="tpu_custom_call" | custom-call | flops 12884901888 | bytes 32505856 | tf_op jit(solution)/shard_map/ladder/pallas_call | solution.py:172
  150.0 1.5 collective-permute-start.12
  151.5 2.5 %collective-permute-start.13 = (bf16[4,24,16,128]{3,2,1,0:T(8,128)(2,1)}, bf16[4,24,16,128]{3,2,1,0:T(8,128)(2,1)}, u32[]{:S(2)}, u32[]{:S(2)}) collective-permute-start(bf16[4,24,16,128]{3,2,1,0:T(8,128)(2,1)} %get-tuple-element.53), channel_id=1, source_target_pairs={{0,16},{1,17},{2,18},{3,19},{4,20},{5,21},{6,22},{7,23},{8,24},{9,... | collective-permute-start | bytes 1179656 | tf_op jit(solution)/shard_map/ppermute | solution.py:219
  154.0 2.7 %fusion.11 = (bf16[4,24,16,128]{3,2,1,0:T(8,128)(2,1)}, bf16[4,24,16,128]{3,2,1,0:T(8,128)(2,1)}, bf16[4,24,16,128]{3,2,1,0:T(8,128)(2,1)}, bf16[4,24,16,128]{3,2,1,0:T(8,128)(2,1)S(1)}) fusion(bf16[2,2,4,24,16,128]{5,4,3,2,1,0:T(8,128)(2,1)S(1)} %collective-permute-done.18, bf16[2,2,4,24,16,128]{5,4,3,2,1,0:T(8,128)(2,1)} %get-tuple-element.57), kind=kLoop, calls=%fused_computation.33 | loop fusion | flops 3145728 | bytes 4718592 | tf_op jit(solution)/shard_map/convert_element_type | solution.py:278
  156.7 12.4 %ladder.5 = (bf16[2,2,4,16,16,128]{5,4,3,2,1,0:T(8,128)(2,1)}, bf16[2,2,4,16,16,128]{5,4,3,2,1,0:T(8,128)(2,1)}) custom-call(s32[4]{0:T(128)} %pad_add_fusion.place_ref, s32[32]{0:T(128)} %reshape.112.mask_ref, bf16[16,2,64,4096]{3,2,1,0:T(8,128)(2,1)} %bitcast.98, bf16[512,4096]{1,0:T(8,128)(2,1)} %all-gather.2.cloned.1.call-done.amps_ref), custom_call_target="tpu_custom_call" | custom-call | flops 8589934592 | bytes 23068672 | tf_op jit(solution)/shard_map/ladder/pallas_call | solution.py:172
  169.2 2.9 %collective-permute-done.14 = bf16[4,24,16,128]{3,2,1,0:T(8,128)(2,1)} collective-permute-done((bf16[4,24,16,128]{3,2,1,0:T(8,128)(2,1)S(1)}, bf16[4,24,16,128]{3,2,1,0:T(8,128)(2,1)}, u32[]{:S(2)}, u32[]{:S(2)}) %collective-permute-start.14) | collective-permute-done | bytes 393248 | tf_op jit(solution)/shard_map/ppermute | solution.py:219
  172.1 1.4 add_convert_fusion.5
  173.5 1.6 collective-permute-start.15
  175.2 2.6 %collective-permute-start.16 = (bf16[24,16,128]{2,1,0:T(8,128)(2,1)S(1)}, bf16[24,16,128]{2,1,0:T(8,128)(2,1)S(1)}, u32[]{:S(2)}, u32[]{:S(2)}) collective-permute-start(bf16[24,16,128]{2,1,0:T(8,128)(2,1)S(1)} %get-tuple-element.86), channel_id=1, source_target_pairs={{0,4},{1,5},{2,6},{3,7},{4,0},{5,1},{6,2},{7,3},{8,12},{9,13},{10,... | collective-permute-start | bytes 294920 | tf_op jit(solution)/shard_map/ppermute | solution.py:219
  177.8 1.3 collective-permute-start.17
  179.4 1.5 collective-permute-start.19
  180.9 0.3 collective-permute-done.15
  181.2 1.7 collective-permute-start.20
  182.9 1.3 collective-permute-done.16
  184.2 2.4 %collective-permute-start.21 = (bf16[4,24,16,128]{3,2,1,0:T(8,128)(2,1)}, bf16[4,24,16,128]{3,2,1,0:T(8,128)(2,1)S(1)}, u32[]{:S(2)}, u32[]{:S(2)}) collective-permute-start(bf16[4,24,16,128]{3,2,1,0:T(8,128)(2,1)} %get-tuple-element.62), channel_id=1, source_target_pairs={{0,17},{1,16},{2,19},{3,18},{4,21},{5,20},{6,23},{7,22},{8,25},{9,... | collective-permute-start | bytes 1179656 | tf_op jit(solution)/shard_map/ppermute | solution.py:219
  186.7 0.2 fusion.13
  186.9 0.6 collective-permute-start.26
  187.5 0.6 collective-permute-start.27
  188.1 5.3 %collective-permute-done.19 = bf16[4,24,16,128]{3,2,1,0:T(8,128)(2,1)S(1)} collective-permute-done((bf16[4,24,16,128]{3,2,1,0:T(8,128)(2,1)}, bf16[4,24,16,128]{3,2,1,0:T(8,128)(2,1)S(1)}, u32[]{:S(2)}, u32[]{:S(2)}) %collective-permute-start.19) | collective-permute-done | bytes 393248 | tf_op jit(solution)/shard_map/ppermute | solution.py:219
  193.4 7.2 %collective-permute-start.28 = (bf16[4,16,16,128]{3,2,1,0:T(8,128)(2,1)S(1)}, bf16[4,16,16,128]{3,2,1,0:T(8,128)(2,1)S(1)}, u32[]{:S(2)}, u32[]{:S(2)}) collective-permute-start(bf16[4,16,16,128]{3,2,1,0:T(8,128)(2,1)S(1)} %get-tuple-element.76), channel_id=1, source_target_pairs={{0,17},{1,16},{2,19},{3,18},{4,21},{5,20},{6,23},{7,22},{8,25},{9,... | collective-permute-start | bytes 786440 | tf_op jit(solution)/shard_map/ppermute | solution.py:219
  200.6 1.9 collective-permute-done.21
  202.8 3.1 %collective-permute-start.22 = (bf16[24,16,128]{2,1,0:T(8,128)(2,1)S(1)}, bf16[24,16,128]{2,1,0:T(8,128)(2,1)S(1)}, u32[]{:S(2)}, u32[]{:S(2)}) collective-permute-start(bf16[24,16,128]{2,1,0:T(8,128)(2,1)S(1)} %get-tuple-element.87), channel_id=1, source_target_pairs={{0,2},{1,3},{2,4},{3,5},{4,6},{5,7},{6,0},{7,1},{8,10},{9,11},{10,... | collective-permute-start | bytes 294920 | tf_op jit(solution)/shard_map/ppermute | solution.py:219
  206.0 2.8 %collective-permute-start.24 = (bf16[24,16,128]{2,1,0:T(8,128)(2,1)S(1)}, bf16[24,16,128]{2,1,0:T(8,128)(2,1)S(1)}, u32[]{:S(2)}, u32[]{:S(2)}) collective-permute-start(bf16[24,16,128]{2,1,0:T(8,128)(2,1)S(1)} %get-tuple-element.88), channel_id=1, source_target_pairs={{0,6},{1,7},{2,0},{3,1},{4,2},{5,3},{6,4},{7,5},{8,14},{9,15},{10,... | collective-permute-start | bytes 294920 | tf_op jit(solution)/shard_map/ppermute | solution.py:219
  208.8 1.6 collective-permute-done.28
  210.7 0.7 collective-permute-start.29
  211.4 1.6 collective-permute-start.30
  212.9 1.6 collective-permute-start.31
  214.7 2.2 collective-permute-done.29
  216.9 1.4 collective-permute-done.30
  218.4 0.8 copy.14
  (61 shorter events, 2.5 us)
Async XLA Ops:
  6.5 103.9 %all-gather.2.cloned.1.call-start = ((), (), s32[]{:S(2)}) async-start(), calls=%async_computation | async-start | bytes 4718592 | tf_op jit(solution)/shard_map/all_gather | solution.py:239
  11.2 1.7 collective-permute-start
  13.0 9.5 %collective-permute-start.1 = (bf16[2,32,2048]{2,1,0:T(8,128)(2,1)S(1)}, bf16[2,32,2048]{2,1,0:T(8,128)(2,1)S(1)}, u32[]{:S(2)}, u32[]{:S(2)}) collective-permute-start(bf16[2,32,2048]{2,1,0:T(8,128)(2,1)S(1)} %get-tuple-element.80), channel_id=1, source_target_pairs={{0,16},{1,17},{2,18},{3,19},{4,20},{5,21},{6,22},{7,23},{8,24},{9,... | collective-permute-start | bytes 786440 | tf_op jit(solution)/shard_map/ppermute | solution.py:219
  30.0 40.6 %copy-start.1 = (bf16[24,32,512]{2,1,0:T(8,128)(2,1)}, bf16[24,32,512]{2,1,0:T(8,128)(2,1)S(1)}, u32[]{:S(2)}) copy-start(bf16[24,32,512]{2,1,0:T(8,128)(2,1)S(1)} %get-tuple-element.42.refs_1_) | copy-start | bytes 2359300
  30.0 19.3 %collective-permute-start.3 = (bf16[24,32,512]{2,1,0:T(8,128)(2,1)}, bf16[24,32,512]{2,1,0:T(8,128)(2,1)}, u32[]{:S(2)}, u32[]{:S(2)}) collective-permute-start(bf16[24,32,512]{2,1,0:T(8,128)(2,1)} %get-tuple-element.78.refs_1_), channel_id=1, source_target_pairs={{0,16},{1,17},{2,18},{3,19},{4,20},{5,21},{6,22},{7,23},{8,24},{9,... | collective-permute-start | bytes 2359304 | tf_op jit(solution)/shard_map/ppermute | solution.py:219
  39.4 11.4 %collective-permute-start.4 = (bf16[24,32,512]{2,1,0:T(8,128)(2,1)}, bf16[24,32,512]{2,1,0:T(8,128)(2,1)}, u32[]{:S(2)}, u32[]{:S(2)}) collective-permute-start(bf16[24,32,512]{2,1,0:T(8,128)(2,1)} %get-tuple-element.78.refs_1_), channel_id=1, source_target_pairs={{0,8},{1,9},{2,10},{3,11},{4,12},{5,13},{6,14},{7,15},{8,0},{9,1},... | collective-permute-start | bytes 2359304 | tf_op jit(solution)/shard_map/ppermute | solution.py:219
  49.3 2.6 %collective-permute-start.5 = (bf16[24,32,512]{2,1,0:T(8,128)(2,1)}, bf16[24,32,512]{2,1,0:T(8,128)(2,1)}, u32[]{:S(2)}, u32[]{:S(2)}) collective-permute-start(bf16[24,32,512]{2,1,0:T(8,128)(2,1)} %collective-permute-done.3.refs_3_), channel_id=1, source_target_pairs={{0,8},{1,9},{2,10},{3,11},{4,12},{5,13},{6,14},{7,15},{8,0},{9,1},... | collective-permute-start | bytes 2359304 | tf_op jit(solution)/shard_map/ppermute | solution.py:219
  49.3 21.3 %collective-permute-start.2 = (bf16[24,32,512]{2,1,0:T(8,128)(2,1)S(1)}, bf16[24,32,512]{2,1,0:T(8,128)(2,1)}, u32[]{:S(2)}, u32[]{:S(2)}) collective-permute-start(bf16[24,32,512]{2,1,0:T(8,128)(2,1)S(1)} %get-tuple-element.42.refs_1_), channel_id=1, source_target_pairs={{0,16},{1,17},{2,18},{3,19},{4,20},{5,21},{6,22},{7,23},{8,24},{9,... | collective-permute-start | bytes 2359304 | tf_op jit(solution)/shard_map/ppermute | solution.py:219
  70.6 2.4 %collective-permute-start.7 = (bf16[24,32,512]{2,1,0:T(8,128)(2,1)S(1)}, bf16[24,32,512]{2,1,0:T(8,128)(2,1)S(1)}, u32[]{:S(2)}, u32[]{:S(2)}) collective-permute-start(bf16[24,32,512]{2,1,0:T(8,128)(2,1)S(1)} %get-tuple-element.42.refs_1_), channel_id=1, source_target_pairs={{0,8},{1,9},{2,10},{3,11},{4,12},{5,13},{6,14},{7,15},{8,0},{9,1},... | collective-permute-start | bytes 2359304 | tf_op jit(solution)/shard_map/ppermute | solution.py:219
  70.8 3.4 %collective-permute-start.8 = (bf16[24,32,512]{2,1,0:T(8,128)(2,1)}, bf16[24,32,512]{2,1,0:T(8,128)(2,1)}, u32[]{:S(2)}, u32[]{:S(2)}) collective-permute-start(bf16[24,32,512]{2,1,0:T(8,128)(2,1)} %collective-permute-done.2.refs_3_), channel_id=1, source_target_pairs={{0,8},{1,9},{2,10},{3,11},{4,12},{5,13},{6,14},{7,15},{8,0},{9,1},... | collective-permute-start | bytes 2359304 | tf_op jit(solution)/shard_map/ppermute | solution.py:219
  71.2 21.8 %copy-start.2 = (bf16[16,32,512]{2,1,0:T(8,128)(2,1)}, bf16[16,32,512]{2,1,0:T(8,128)(2,1)S(1)}, u32[]{:S(2)}) copy-start(bf16[16,32,512]{2,1,0:T(8,128)(2,1)S(1)} %slice.90.refs_1_) | copy-start | bytes 1572868
  71.2 22.2 %copy-start.3 = (s32[8,2,2]{0,2,1:T(2,128)S(1)}, s32[8,2,2]{0,2,1:T(2,128)}, u32[]{:S(2)}) copy-start(s32[8,2,2]{0,2,1:T(2,128)} %param.5) | copy-start | bytes 388
  71.2 21.6 %collective-permute-start.6 = (bf16[16,32,512]{2,1,0:T(8,128)(2,1)S(1)}, bf16[16,32,512]{2,1,0:T(8,128)(2,1)S(1)}, u32[]{:S(2)}, u32[]{:S(2)}) collective-permute-start(bf16[16,32,512]{2,1,0:T(8,128)(2,1)S(1)} %slice.90.refs_1_), channel_id=1, source_target_pairs={{0,16},{1,17},{2,18},{3,19},{4,20},{5,21},{6,22},{7,23},{8,24},{9,... | collective-permute-start | bytes 1572872 | tf_op jit(solution)/shard_map/ppermute | solution.py:219
  72.9 0.9 copy-start.4
  92.8 2.7 %copy-start.5 = (bf16[16,32,512]{2,1,0:T(8,128)(2,1)}, bf16[16,32,512]{2,1,0:T(8,128)(2,1)S(1)}, u32[]{:S(2)}) copy-start(bf16[16,32,512]{2,1,0:T(8,128)(2,1)S(1)} %collective-permute-done.6.refs_3_) | copy-start | bytes 1572868
  92.8 2.0 collective-permute-start.10
  93.0 2.5 %collective-permute-start.9 = (bf16[16,32,512]{2,1,0:T(8,128)(2,1)S(1)}, bf16[16,32,512]{2,1,0:T(8,128)(2,1)S(1)}, u32[]{:S(2)}, u32[]{:S(2)}) collective-permute-start(bf16[16,32,512]{2,1,0:T(8,128)(2,1)S(1)} %slice.90.refs_1_), channel_id=1, source_target_pairs={{0,8},{1,9},{2,10},{3,11},{4,12},{5,13},{6,14},{7,15},{8,0},{9,1},... | collective-permute-start | bytes 1572872 | tf_op jit(solution)/shard_map/ppermute | solution.py:219
  94.8 0.8 copy-start.6
  95.6 0.8 copy-start.7
  126.9 3.6 %collective-permute-start.11 = (bf16[2,2,4,24,16,128]{5,4,3,2,1,0:T(8,128)(2,1)}, bf16[2,2,4,24,16,128]{5,4,3,2,1,0:T(8,128)(2,1)S(1)}, u32[]{:S(2)}, u32[]{:S(2)}) collective-permute-start(bf16[2,2,4,24,16,128]{5,4,3,2,1,0:T(8,128)(2,1)} %get-tuple-element.50), channel_id=1, source_target_pairs={{0,8},{1,9},{2,10},{3,11},{4,12},{5,13},{6,14},{7,15},{8,0},{9,1},... | collective-permute-start | bytes 4718600 | tf_op jit(solution)/shard_map/ppermute | solution.py:219
  149.9 4.1 %collective-permute-start.18 = (bf16[2,2,4,24,16,128]{5,4,3,2,1,0:T(8,128)(2,1)}, bf16[2,2,4,24,16,128]{5,4,3,2,1,0:T(8,128)(2,1)S(1)}, u32[]{:S(2)}, u32[]{:S(2)}) collective-permute-start(bf16[2,2,4,24,16,128]{5,4,3,2,1,0:T(8,128)(2,1)} %get-tuple-element.58), channel_id=1, source_target_pairs={{0,8},{1,9},{2,10},{3,11},{4,12},{5,13},{6,14},{7,15},{8,0},{9,1},... | collective-permute-start | bytes 4718600 | tf_op jit(solution)/shard_map/ppermute | solution.py:219
  150.0 19.1 %collective-permute-start.12 = (bf16[4,24,16,128]{3,2,1,0:T(8,128)(2,1)}, bf16[4,24,16,128]{3,2,1,0:T(8,128)(2,1)}, u32[]{:S(2)}, u32[]{:S(2)}) collective-permute-start(bf16[4,24,16,128]{3,2,1,0:T(8,128)(2,1)} %get-tuple-element.52), channel_id=1, source_target_pairs={{0,1},{1,0},{2,3},{3,2},{4,5},{5,4},{6,7},{7,6},{8,9},{9,8},{10,11... | collective-permute-start | bytes 1179656 | tf_op jit(solution)/shard_map/ppermute | solution.py:219
  151.5 17.6 %collective-permute-start.13 = (bf16[4,24,16,128]{3,2,1,0:T(8,128)(2,1)}, bf16[4,24,16,128]{3,2,1,0:T(8,128)(2,1)}, u32[]{:S(2)}, u32[]{:S(2)}) collective-permute-start(bf16[4,24,16,128]{3,2,1,0:T(8,128)(2,1)} %get-tuple-element.53), channel_id=1, source_target_pairs={{0,16},{1,17},{2,18},{3,19},{4,20},{5,21},{6,22},{7,23},{8,24},{9,... | collective-permute-start | bytes 1179656 | tf_op jit(solution)/shard_map/ppermute | solution.py:219
  154.0 18.0 %collective-permute-start.14 = (bf16[4,24,16,128]{3,2,1,0:T(8,128)(2,1)S(1)}, bf16[4,24,16,128]{3,2,1,0:T(8,128)(2,1)}, u32[]{:S(2)}, u32[]{:S(2)}) collective-permute-start(bf16[4,24,16,128]{3,2,1,0:T(8,128)(2,1)S(1)} %get-tuple-element.54), channel_id=1, source_target_pairs={{0,17},{1,16},{2,19},{3,18},{4,21},{5,20},{6,23},{7,22},{8,25},{9,... | collective-permute-start | bytes 1179656 | tf_op jit(solution)/shard_map/ppermute | solution.py:219
  169.2 17.5 %collective-permute-start.25 = (bf16[2,2,4,16,16,128]{5,4,3,2,1,0:T(8,128)(2,1)}, bf16[2,2,4,16,16,128]{5,4,3,2,1,0:T(8,128)(2,1)S(1)}, u32[]{:S(2)}, u32[]{:S(2)}) collective-permute-start(bf16[2,2,4,16,16,128]{5,4,3,2,1,0:T(8,128)(2,1)} %get-tuple-element.66), channel_id=1, source_target_pairs={{0,8},{1,9},{2,10},{3,11},{4,12},{5,13},{6,14},{7,15},{8,0},{9,1},... | collective-permute-start | bytes 3145736 | tf_op jit(solution)/shard_map/ppermute | solution.py:219
  169.2 17.5 %copy-start = (bf16[2,2,4,16,16,128]{5,4,3,2,1,0:T(8,128)(2,1)S(1)}, bf16[2,2,4,16,16,128]{5,4,3,2,1,0:T(8,128)(2,1)}, u32[]{:S(2)}) copy-start(bf16[2,2,4,16,16,128]{5,4,3,2,1,0:T(8,128)(2,1)} %get-tuple-element.65) | copy-start | bytes 3145732
  173.5 7.6 %collective-permute-start.15 = (bf16[24,16,128]{2,1,0:T(8,128)(2,1)S(1)}, bf16[24,16,128]{2,1,0:T(8,128)(2,1)S(1)}, u32[]{:S(2)}, u32[]{:S(2)}) collective-permute-start(bf16[24,16,128]{2,1,0:T(8,128)(2,1)S(1)} %get-tuple-element.84), channel_id=1, source_target_pairs={{0,2},{1,3},{2,4},{3,5},{4,6},{5,7},{6,0},{7,1},{8,10},{9,11},{10,... | collective-permute-start | bytes 294920 | tf_op jit(solution)/shard_map/ppermute | solution.py:219
  175.2 9.0 %collective-permute-start.16 = (bf16[24,16,128]{2,1,0:T(8,128)(2,1)S(1)}, bf16[24,16,128]{2,1,0:T(8,128)(2,1)S(1)}, u32[]{:S(2)}, u32[]{:S(2)}) collective-permute-start(bf16[24,16,128]{2,1,0:T(8,128)(2,1)S(1)} %get-tuple-element.86), channel_id=1, source_target_pairs={{0,4},{1,5},{2,6},{3,7},{4,0},{5,1},{6,2},{7,3},{8,12},{9,13},{10,... | collective-permute-start | bytes 294920 | tf_op jit(solution)/shard_map/ppermute | solution.py:219
  177.8 8.8 %collective-permute-start.17 = (bf16[24,16,128]{2,1,0:T(8,128)(2,1)S(1)}, bf16[24,16,128]{2,1,0:T(8,128)(2,1)S(1)}, u32[]{:S(2)}, u32[]{:S(2)}) collective-permute-start(bf16[24,16,128]{2,1,0:T(8,128)(2,1)S(1)} %get-tuple-element.85), channel_id=1, source_target_pairs={{0,6},{1,7},{2,0},{3,1},{4,2},{5,3},{6,4},{7,5},{8,14},{9,15},{10,... | collective-permute-start | bytes 294920 | tf_op jit(solution)/shard_map/ppermute | solution.py:219
  179.4 14.0 %collective-permute-start.19 = (bf16[4,24,16,128]{3,2,1,0:T(8,128)(2,1)}, bf16[4,24,16,128]{3,2,1,0:T(8,128)(2,1)S(1)}, u32[]{:S(2)}, u32[]{:S(2)}) collective-permute-start(bf16[4,24,16,128]{3,2,1,0:T(8,128)(2,1)} %get-tuple-element.60), channel_id=1, source_target_pairs={{0,1},{1,0},{2,3},{3,2},{4,5},{5,4},{6,7},{7,6},{8,9},{9,8},{10,11... | collective-permute-start | bytes 1179656 | tf_op jit(solution)/shard_map/ppermute | solution.py:219
  181.2 19.4 %collective-permute-start.20 = (bf16[4,24,16,128]{3,2,1,0:T(8,128)(2,1)}, bf16[4,24,16,128]{3,2,1,0:T(8,128)(2,1)S(1)}, u32[]{:S(2)}, u32[]{:S(2)}) collective-permute-start(bf16[4,24,16,128]{3,2,1,0:T(8,128)(2,1)} %get-tuple-element.61), channel_id=1, source_target_pairs={{0,16},{1,17},{2,18},{3,19},{4,20},{5,21},{6,22},{7,23},{8,24},{9,... | collective-permute-start | bytes 1179656 | tf_op jit(solution)/shard_map/ppermute | solution.py:219
  184.2 18.3 %collective-permute-start.21 = (bf16[4,24,16,128]{3,2,1,0:T(8,128)(2,1)}, bf16[4,24,16,128]{3,2,1,0:T(8,128)(2,1)S(1)}, u32[]{:S(2)}, u32[]{:S(2)}) collective-permute-start(bf16[4,24,16,128]{3,2,1,0:T(8,128)(2,1)} %get-tuple-element.62), channel_id=1, source_target_pairs={{0,17},{1,16},{2,19},{3,18},{4,21},{5,20},{6,23},{7,22},{8,25},{9,... | collective-permute-start | bytes 1179656 | tf_op jit(solution)/shard_map/ppermute | solution.py:219
  186.9 19.0 %collective-permute-start.26 = (bf16[4,16,16,128]{3,2,1,0:T(8,128)(2,1)S(1)}, bf16[4,16,16,128]{3,2,1,0:T(8,128)(2,1)S(1)}, u32[]{:S(2)}, u32[]{:S(2)}) collective-permute-start(bf16[4,16,16,128]{3,2,1,0:T(8,128)(2,1)S(1)} %get-tuple-element.75), channel_id=1, source_target_pairs={{0,1},{1,0},{2,3},{3,2},{4,5},{5,4},{6,7},{7,6},{8,9},{9,8},{10,11... | collective-permute-start | bytes 786440 | tf_op jit(solution)/shard_map/ppermute | solution.py:219
  187.5 21.3 %collective-permute-start.27 = (bf16[4,16,16,128]{3,2,1,0:T(8,128)(2,1)S(1)}, bf16[4,16,16,128]{3,2,1,0:T(8,128)(2,1)S(1)}, u32[]{:S(2)}, u32[]{:S(2)}) collective-permute-start(bf16[4,16,16,128]{3,2,1,0:T(8,128)(2,1)S(1)} %get-tuple-element.77), channel_id=1, source_target_pairs={{0,16},{1,17},{2,18},{3,19},{4,20},{5,21},{6,22},{7,23},{8,24},{9,... | collective-permute-start | bytes 786440 | tf_op jit(solution)/shard_map/ppermute | solution.py:219
  193.4 17.0 %collective-permute-start.28 = (bf16[4,16,16,128]{3,2,1,0:T(8,128)(2,1)S(1)}, bf16[4,16,16,128]{3,2,1,0:T(8,128)(2,1)S(1)}, u32[]{:S(2)}, u32[]{:S(2)}) collective-permute-start(bf16[4,16,16,128]{3,2,1,0:T(8,128)(2,1)S(1)} %get-tuple-element.76), channel_id=1, source_target_pairs={{0,17},{1,16},{2,19},{3,18},{4,21},{5,20},{6,23},{7,22},{8,25},{9,... | collective-permute-start | bytes 786440 | tf_op jit(solution)/shard_map/ppermute | solution.py:219
  202.8 10.2 %collective-permute-start.22 = (bf16[24,16,128]{2,1,0:T(8,128)(2,1)S(1)}, bf16[24,16,128]{2,1,0:T(8,128)(2,1)S(1)}, u32[]{:S(2)}, u32[]{:S(2)}) collective-permute-start(bf16[24,16,128]{2,1,0:T(8,128)(2,1)S(1)} %get-tuple-element.87), channel_id=1, source_target_pairs={{0,2},{1,3},{2,4},{3,5},{4,6},{5,7},{6,0},{7,1},{8,10},{9,11},{10,... | collective-permute-start | bytes 294920 | tf_op jit(solution)/shard_map/ppermute | solution.py:219
  205.8 8.9 %collective-permute-start.23 = (bf16[24,16,128]{2,1,0:T(8,128)(2,1)S(1)}, bf16[24,16,128]{2,1,0:T(8,128)(2,1)S(1)}, u32[]{:S(2)}, u32[]{:S(2)}) collective-permute-start(bf16[24,16,128]{2,1,0:T(8,128)(2,1)S(1)} %get-tuple-element.89), channel_id=1, source_target_pairs={{0,4},{1,5},{2,6},{3,7},{4,0},{5,1},{6,2},{7,3},{8,12},{9,13},{10,... | collective-permute-start | bytes 294920 | tf_op jit(solution)/shard_map/ppermute | solution.py:219
  206.0 8.7 %collective-permute-start.24 = (bf16[24,16,128]{2,1,0:T(8,128)(2,1)S(1)}, bf16[24,16,128]{2,1,0:T(8,128)(2,1)S(1)}, u32[]{:S(2)}, u32[]{:S(2)}) collective-permute-start(bf16[24,16,128]{2,1,0:T(8,128)(2,1)S(1)} %get-tuple-element.88), channel_id=1, source_target_pairs={{0,6},{1,7},{2,0},{3,1},{4,2},{5,3},{6,4},{7,5},{8,14},{9,15},{10,... | collective-permute-start | bytes 294920 | tf_op jit(solution)/shard_map/ppermute | solution.py:219
  210.7 6.2 %collective-permute-start.29 = (bf16[16,16,128]{2,1,0:T(8,128)(2,1)S(1)}, bf16[16,16,128]{2,1,0:T(8,128)(2,1)S(1)}, u32[]{:S(2)}, u32[]{:S(2)}) collective-permute-start(bf16[16,16,128]{2,1,0:T(8,128)(2,1)S(1)} %get-tuple-element.90), channel_id=1, source_target_pairs={{0,2},{1,3},{2,4},{3,5},{4,6},{5,7},{6,0},{7,1},{8,10},{9,11},{10,... | collective-permute-start | bytes 196616 | tf_op jit(solution)/shard_map/ppermute | solution.py:219
  211.4 7.0 %collective-permute-start.30 = (bf16[16,16,128]{2,1,0:T(8,128)(2,1)S(1)}, bf16[16,16,128]{2,1,0:T(8,128)(2,1)S(1)}, u32[]{:S(2)}, u32[]{:S(2)}) collective-permute-start(bf16[16,16,128]{2,1,0:T(8,128)(2,1)S(1)} %get-tuple-element.92), channel_id=1, source_target_pairs={{0,4},{1,5},{2,6},{3,7},{4,0},{5,1},{6,2},{7,3},{8,12},{9,13},{10,... | collective-permute-start | bytes 196616 | tf_op jit(solution)/shard_map/ppermute | solution.py:219
  212.9 5.4 %collective-permute-start.31 = (bf16[16,16,128]{2,1,0:T(8,128)(2,1)S(1)}, bf16[16,16,128]{2,1,0:T(8,128)(2,1)S(1)}, u32[]{:S(2)}, u32[]{:S(2)}) collective-permute-start(bf16[16,16,128]{2,1,0:T(8,128)(2,1)S(1)} %get-tuple-element.91), channel_id=1, source_target_pairs={{0,6},{1,7},{2,0},{3,1},{4,2},{5,3},{6,4},{7,5},{8,14},{9,15},{10,... | collective-permute-start | bytes 196616 | tf_op jit(solution)/shard_map/ppermute | solution.py:219
Sparse Core Ops, SparseCore 0:
  29.1 74.2 all-gather.1

commit v3 on v2

--- a/solution.py
+++ b/solution.py
@@ -73,7 +73,7 @@
 
 
 def tiled_ladder_kernel(
-    place_ref, mask_ref, integrals_ref, amps_ref, keep_ref, send_ref, list_ref, full_ref
+    place_ref, mask_ref, integrals_ref, amps_ref, keep_ref, send_ref, list_ref, full_ref, some_ref
 ):
     high, inner, outer, bs, a_local, quarter = keep_ref.shape
     low = 2
@@ -82,7 +82,7 @@
     v_blocks = mask_ref.shape[0] // slots
     wide = round(v_blocks**0.5)
     core, chip_x, near, c_block = (place_ref[i] for i in range(4))
-    a_at = pl.program_id(1)
+    a_at = pl.program_id(0)
 
     listed = jnp.int32(0)
     for n in range(slots):
@@ -116,13 +116,16 @@
 
     @pl.when(listed <= few)
     def _():
-        full_ref[...] = jnp.zeros_like(full_ref)
         at = [list_ref[n] for n in range(few)]
-        some = product(
-            jnp.concatenate(
-                [amps_ref[pl.ds(pl.multiple_of(n * IJB, IJB), IJB), :] for n in at], axis=0
-            )
-        )
+
+        @pl.when(pl.program_id(1) == 0)
+        def _():
+            full_ref[...] = jnp.zeros_like(full_ref)
+            for n, index in enumerate(at):
+                start = pl.multiple_of(index * IJB, IJB)
+                some_ref[n * IJB : (n + 1) * IJB, :] = amps_ref[pl.ds(start, IJB), :]
+
+        some = product(some_ref[...])
         per = quarter // IJB
         for n, index in enumerate(at):
             for k in range(per):
@@ -158,15 +161,16 @@
         spec = pl.BlockSpec((high, block, quarter), lambda i, j, *_: (0, i, 0))
     else:
         bs, parts = ROW_BLOCK // VB, a_all // VB
-        kernel, grid = tiled_ladder_kernel, (rows // a_all // bs, parts)
+        kernel, grid = tiled_ladder_kernel, (parts, rows // a_all // bs)
         integrals = integrals.reshape(rows // a_all, parts, VB, inner)
-        left_spec = pl.BlockSpec((bs, 1, VB, inner), lambda i, j, *_: (i, j, 0, 0))
+        left_spec = pl.BlockSpec((bs, 1, VB, inner), lambda j, i, *_: (i, j, 0, 0))
         shape = (high, near, far, rows // a_all, a_local, quarter)
         piece = (high, near, far // parts, bs, a_local, quarter)
-        spec = pl.BlockSpec(piece, lambda i, j, *_: (0, 0, j, i, 0, 0))
+        spec = pl.BlockSpec(piece, lambda j, i, *_: (0, 0, j, i, 0, 0))
         scratch = [
             pltpu.SMEM((pairs // IJB,), jnp.int32),
             pltpu.VMEM((high * low, bs * VB, quarter), jnp.bfloat16),
+            pltpu.VMEM((pairs // 2, inner), jnp.bfloat16),
         ]
     shape = jax.ShapeDtypeStruct(shape, jnp.bfloat16)
     return pl.pallas_call(

time: 227 us -> 227 us (level)
  transfers between devices with their start and end apart: 33 -> 33, of which waited for: 17 -> 16; matrix products, arithmetic and copies ran while one was open for 9% -> 9% of each run, Pallas kernels for 28% -> 28%
where the time goes in v3:
time: 227 us; the launch traced here: 226 us
  Pallas kernels  97.6 us (43%)
  starting transfers between devices  42.9 us (19%)
  waiting for transfers between devices  34.6 us (15%)
  local copies, waits for them, and re-layouts  26.4 us (12%)
  between operations  13.6 us (6%)
  other arithmetic  11.2 us (5%)
    pallas_call x3, Pallas kernels, partial_integrals(): pl.pallas_call(integrals_kernel, grid=(c_all // CGROUP,), in_specs=[pl.Bl...  51.3 us
    pallas_call x3, Pallas kernels, ladder(): pl.pallas_call(kernel, grid_spec=pltpu.PrefetchScalarGridSpec(num_scalar_...  46.4 us
    ppermute x32, starting transfers between devices, shift(): return lax.ppermute(x, ('grp', 'tile'), pairs_of)  42.9 us
    ppermute x32, waiting for transfers between devices, shift(): return lax.ppermute(x, ('grp', 'tile'), pairs_of)  34.5 us
    unnamed x19, local copies, waits for them, and re-layouts  15.4 us
    convert_element_type x3, other arithmetic, on_device(): parts.append((halves[0].astype(f32) + halves[1].astype(f32)).astype(bf16))  5.61 us
  transfers between devices with their start and end apart: 33, of which 16 were waited for; matrix products, arithmetic and copies ran while one was open for 9% of the time, Pallas kernels for 28%

profile of v3, /device:TPU:0, one launch (start us, length us, event | category | flops | bytes accessed | tf_op | source)
XLA Modules:
  0.0 226.2 jit_solution(9550577558451987013)
XLA Ops:
  6.5 0.9 fusion.30
  7.6 1.1 multiply_bitcast_fusion
  8.6 1.7 copy.9
  10.3 0.8 reshape.108
  11.2 0.6 collective-permute-start
  11.8 1.2 collective-permute-done
  13.0 2.9 %collective-permute-start.1 = (bf16[2,32,2048]{2,1,0:T(8,128)(2,1)S(1)}, bf16[2,32,2048]{2,1,0:T(8,128)(2,1)S(1)}, u32[]{:S(2)}, u32[]{:S(2)}) collective-permute-start(bf16[2,32,2048]{2,1,0:T(8,128)(2,1)S(1)} %get-tuple-element.80), channel_id=1, source_target_pairs={{0,16},{1,17},{2,18},{3,19},{4,20},{5,21},{6,22},{7,23},{8,24},{9,... | collective-permute-start | bytes 786440 | tf_op jit(solution)/shard_map/ppermute | solution.py:223
  15.9 5.8 %copy.15 = bf16[512,32,64]{0,1,2:T(8,128)(2,1)S(1)} copy(bf16[512,32,64]{2,1,0:T(8,128)(2,1)} %bitcast.87) | data formatting | bytes 4194304
  21.7 0.8 collective-permute-done.1
  22.5 0.8 pad_maximum_fusion
  23.3 2.1 reshape.109
  25.4 1.1 copy.10
  26.6 2.4 %copy.11 = bf16[64,4096]{1,0:T(8,128)(2,1)} copy(bf16[64,4096]{0,1:T(8,128)(2,1)} %bitcast.94) | data formatting | bytes 1048576 | tf_op jit(solution)/shard_map/reshape | solution.py:242
  28.9 1.0 fusion.33
  30.0 1.7 collective-permute-start.3
  31.7 7.6 %copy.12 = bf16[512,32,128]{0,2,1:T(8,128)(2,1)} copy(bf16[512,32,128]{2,1,0:T(8,128)(2,1)} %param.3) | data formatting | bytes 8388608 | tf_op args[0]
  39.4 9.9 %collective-permute-done.3.refs_3_ = bf16[24,32,512]{2,1,0:T(8,128)(2,1)} collective-permute-done((bf16[24,32,512]{2,1,0:T(8,128)(2,1)}, bf16[24,32,512]{2,1,0:T(8,128)(2,1)}, u32[]{:S(2)}, u32[]{:S(2)}) %collective-permute-start.3) | collective-permute-done | bytes 786464 | tf_op jit(solution)/shard_map/ppermute | solution.py:223
  49.3 1.5 collective-permute-start.2
  50.8 1.2 collective-permute-done.5.refs_4_
  51.9 18.6 %partial_integrals.3 = bf16[3072,4096]{1,0:T(8,128)(2,1)} custom-call(bf16[4096,512]{1,0:T(8,128)(2,1)} %bitcast.90, bf16[24,32,512]{2,1,0:T(8,128)(2,1)} %get-tuple-element.78.refs_1_, bf16[24,32,512]{2,1,0:T(8,128)(2,1)} %collective-permute-done.4.refs_2_, bf16[24,32,512]{2,1,0:T(8,128)(2,1)} %collective-permute-done.3.refs_3_, ...), custom_call_target="tpu_custom_call" | custom-call | flops 12884901888 | bytes 32505856 | tf_op jit(solution)/shard_map/partial_integrals/pallas_call | solution.py:43
  70.8 0.4 collective-permute-start.8
  71.2 1.5 collective-permute-start.6
  72.9 0.9 copy-done.4
  73.8 0.3 collective-permute-done.8.refs_4_
  74.2 18.6 %partial_integrals.4 = bf16[3072,4096]{1,0:T(8,128)(2,1)} custom-call(bf16[4096,512]{1,0:T(8,128)(2,1)} %bitcast.91, bf16[24,32,512]{2,1,0:T(8,128)(2,1)} %copy-done.1, bf16[24,32,512]{2,1,0:T(8,128)(2,1)} %copy-done.4, bf16[24,32,512]{2,1,0:T(8,128)(2,1)} %collective-permute-done.2.refs_3_, bf16[24,32,512]{2,1,0:T(8,128)(2,1)} %collective-permute-done.8.refs_4_), custom_call_target="tpu_custom_call" | custom-call | flops 12884901888 | bytes 32505856 | tf_op jit(solution)/shard_map/partial_integrals/pallas_call | solution.py:43
  93.0 0.4 collective-permute-start.9
  93.5 0.6 reshape.112.mask_ref
  94.1 0.7 pad_add_fusion.place_ref
  94.8 0.7 collective-permute-done.9.refs_2_
  95.6 0.8 copy-done.7
  96.4 14.0 %partial_integrals.5 = bf16[2048,4096]{1,0:T(8,128)(2,1)} custom-call(bf16[4096,512]{1,0:T(8,128)(2,1)} %bitcast.92, bf16[16,32,512]{2,1,0:T(8,128)(2,1)} %copy-done.2, bf16[16,32,512]{2,1,0:T(8,128)(2,1)} %copy-done.7, bf16[16,32,512]{2,1,0:T(8,128)(2,1)} %copy-done.5, bf16[16,32,512]{2,1,0:T(8,128)(2,1)} %copy-done.6), custom_call_target="tpu_custom_call" | custom-call | flops 8589934592 | bytes 23068672 | tf_op jit(solution)/shard_map/partial_integrals/pallas_call | solution.py:43
  110.4 16.8 %ladder.3 = (bf16[2,2,4,24,16,128]{5,4,3,2,1,0:T(8,128)(2,1)}, bf16[2,2,4,24,16,128]{5,4,3,2,1,0:T(8,128)(2,1)}) custom-call(s32[4]{0:T(128)} %pad_add_fusion.place_ref, s32[32]{0:T(128)} %reshape.112.mask_ref, bf16[24,2,64,4096]{3,2,1,0:T(8,128)(2,1)} %bitcast.96, bf16[512,4096]{1,0:T(8,128)(2,1)} %all-gather.2.cloned.1.call-done.amps_ref), custom_call_target="tpu_custom_call" | custom-call | flops 12884901888 | bytes 32505856 | tf_op jit(solution)/shard_map/ladder/pallas_call | solution.py:176
  127.3 3.5 %collective-permute-done.11 = bf16[2,2,4,24,16,128]{5,4,3,2,1,0:T(8,128)(2,1)S(1)} collective-permute-done((bf16[2,2,4,24,16,128]{5,4,3,2,1,0:T(8,128)(2,1)}, bf16[2,2,4,24,16,128]{5,4,3,2,1,0:T(8,128)(2,1)S(1)}, u32[]{:S(2)}, u32[]{:S(2)}) %collective-permute-start.11) | collective-permute-done | bytes 1572896 | tf_op jit(solution)/shard_map/ppermute | solution.py:223
  130.8 2.7 %fusion.7 = (bf16[4,24,16,128]{3,2,1,0:T(8,128)(2,1)S(1)}, bf16[4,24,16,128]{3,2,1,0:T(8,128)(2,1)}, bf16[4,24,16,128]{3,2,1,0:T(8,128)(2,1)}, bf16[4,24,16,128]{3,2,1,0:T(8,128)(2,1)S(1)}) fusion(bf16[2,2,4,24,16,128]{5,4,3,2,1,0:T(8,128)(2,1)S(1)} %collective-permute-done.11, bf16[2,2,4,24,16,128]{5,4,3,2,1,0:T(8,128)(2,1)} %get-tuple-element.49), kind=kLoop, calls=%fused_computation.29 | loop fusion | flops 3145728 | bytes 4718592 | tf_op jit(solution)/shard_map/convert_element_type | solution.py:282
  133.5 17.0 %ladder.4 = (bf16[2,2,4,24,16,128]{5,4,3,2,1,0:T(8,128)(2,1)}, bf16[2,2,4,24,16,128]{5,4,3,2,1,0:T(8,128)(2,1)}) custom-call(s32[4]{0:T(128)} %pad_add_fusion.place_ref, s32[32]{0:T(128)} %reshape.112.mask_ref, bf16[24,2,64,4096]{3,2,1,0:T(8,128)(2,1)} %bitcast.97, bf16[512,4096]{1,0:T(8,128)(2,1)} %all-gather.2.cloned.1.call-done.amps_ref), custom_call_target="tpu_custom_call" | custom-call | flops 12884901888 | bytes 32505856 | tf_op jit(solution)/shard_map/ladder/pallas_call | solution.py:176
  150.6 1.5 collective-permute-start.12
  152.1 2.2 collective-permute-start.13
  154.3 2.7 %fusion.11 = (bf16[4,24,16,128]{3,2,1,0:T(8,128)(2,1)}, bf16[4,24,16,128]{3,2,1,0:T(8,128)(2,1)}, bf16[4,24,16,128]{3,2,1,0:T(8,128)(2,1)}, bf16[4,24,16,128]{3,2,1,0:T(8,128)(2,1)S(1)}) fusion(bf16[2,2,4,24,16,128]{5,4,3,2,1,0:T(8,128)(2,1)S(1)} %collective-permute-done.18, bf16[2,2,4,24,16,128]{5,4,3,2,1,0:T(8,128)(2,1)} %get-tuple-element.57), kind=kLoop, calls=%fused_computation.33 | loop fusion | flops 3145728 | bytes 4718592 | tf_op jit(solution)/shard_map/convert_element_type | solution.py:282
  157.0 12.6 %ladder.5 = (bf16[2,2,4,16,16,128]{5,4,3,2,1,0:T(8,128)(2,1)}, bf16[2,2,4,16,16,128]{5,4,3,2,1,0:T(8,128)(2,1)}) custom-call(s32[4]{0:T(128)} %pad_add_fusion.place_ref, s32[32]{0:T(128)} %reshape.112.mask_ref, bf16[16,2,64,4096]{3,2,1,0:T(8,128)(2,1)} %bitcast.98, bf16[512,4096]{1,0:T(8,128)(2,1)} %all-gather.2.cloned.1.call-done.amps_ref), custom_call_target="tpu_custom_call" | custom-call | flops 8589934592 | bytes 23068672 | tf_op jit(solution)/shard_map/ladder/pallas_call | solution.py:176
  169.7 2.7 %collective-permute-done.14 = bf16[4,24,16,128]{3,2,1,0:T(8,128)(2,1)} collective-permute-done((bf16[4,24,16,128]{3,2,1,0:T(8,128)(2,1)S(1)}, bf16[4,24,16,128]{3,2,1,0:T(8,128)(2,1)}, u32[]{:S(2)}, u32[]{:S(2)}) %collective-permute-start.14) | collective-permute-done | bytes 393248 | tf_op jit(solution)/shard_map/ppermute | solution.py:223
  172.4 1.4 add_convert_fusion.5
  173.9 1.6 collective-permute-start.15
  175.5 2.6 %collective-permute-start.16 = (bf16[24,16,128]{2,1,0:T(8,128)(2,1)S(1)}, bf16[24,16,128]{2,1,0:T(8,128)(2,1)S(1)}, u32[]{:S(2)}, u32[]{:S(2)}) collective-permute-start(bf16[24,16,128]{2,1,0:T(8,128)(2,1)S(1)} %get-tuple-element.86), channel_id=1, source_target_pairs={{0,4},{1,5},{2,6},{3,7},{4,0},{5,1},{6,2},{7,3},{8,12},{9,13},{10,... | collective-permute-start | bytes 294920 | tf_op jit(solution)/shard_map/ppermute | solution.py:223
  178.1 1.3 collective-permute-start.17
  179.7 1.5 collective-permute-start.19
  181.2 0.3 collective-permute-done.15
  181.5 1.7 collective-permute-start.20
  183.2 1.3 collective-permute-done.16
  184.5 2.4 %collective-permute-start.21 = (bf16[4,24,16,128]{3,2,1,0:T(8,128)(2,1)}, bf16[4,24,16,128]{3,2,1,0:T(8,128)(2,1)S(1)}, u32[]{:S(2)}, u32[]{:S(2)}) collective-permute-start(bf16[4,24,16,128]{3,2,1,0:T(8,128)(2,1)} %get-tuple-element.62), channel_id=1, source_target_pairs={{0,17},{1,16},{2,19},{3,18},{4,21},{5,20},{6,23},{7,22},{8,25},{9,... | collective-permute-start | bytes 1179656 | tf_op jit(solution)/shard_map/ppermute | solution.py:223
  187.2 0.6 collective-permute-start.26
  187.8 0.6 collective-permute-start.27
  188.4 5.3 %collective-permute-done.19 = bf16[4,24,16,128]{3,2,1,0:T(8,128)(2,1)S(1)} collective-permute-done((bf16[4,24,16,128]{3,2,1,0:T(8,128)(2,1)}, bf16[4,24,16,128]{3,2,1,0:T(8,128)(2,1)S(1)}, u32[]{:S(2)}, u32[]{:S(2)}) %collective-permute-start.19) | collective-permute-done | bytes 393248 | tf_op jit(solution)/shard_map/ppermute | solution.py:223
  193.7 7.2 %collective-permute-start.28 = (bf16[4,16,16,128]{3,2,1,0:T(8,128)(2,1)S(1)}, bf16[4,16,16,128]{3,2,1,0:T(8,128)(2,1)S(1)}, u32[]{:S(2)}, u32[]{:S(2)}) collective-permute-start(bf16[4,16,16,128]{3,2,1,0:T(8,128)(2,1)S(1)} %get-tuple-element.76), channel_id=1, source_target_pairs={{0,17},{1,16},{2,19},{3,18},{4,21},{5,20},{6,23},{7,22},{8,25},{9,... | collective-permute-start | bytes 786440 | tf_op jit(solution)/shard_map/ppermute | solution.py:223
  200.9 1.9 collective-permute-done.21
  203.0 2.9 %collective-permute-start.22 = (bf16[24,16,128]{2,1,0:T(8,128)(2,1)S(1)}, bf16[24,16,128]{2,1,0:T(8,128)(2,1)S(1)}, u32[]{:S(2)}, u32[]{:S(2)}) collective-permute-start(bf16[24,16,128]{2,1,0:T(8,128)(2,1)S(1)} %get-tuple-element.87), channel_id=1, source_target_pairs={{0,2},{1,3},{2,4},{3,5},{4,6},{5,7},{6,0},{7,1},{8,10},{9,11},{10,... | collective-permute-start | bytes 294920 | tf_op jit(solution)/shard_map/ppermute | solution.py:223
  205.9 0.3 collective-permute-start.23
  206.3 2.8 %collective-permute-start.24 = (bf16[24,16,128]{2,1,0:T(8,128)(2,1)S(1)}, bf16[24,16,128]{2,1,0:T(8,128)(2,1)S(1)}, u32[]{:S(2)}, u32[]{:S(2)}) collective-permute-start(bf16[24,16,128]{2,1,0:T(8,128)(2,1)S(1)} %get-tuple-element.88), channel_id=1, source_target_pairs={{0,6},{1,7},{2,0},{3,1},{4,2},{5,3},{6,4},{7,5},{8,14},{9,15},{10,... | collective-permute-start | bytes 294920 | tf_op jit(solution)/shard_map/ppermute | solution.py:223
  209.1 1.6 collective-permute-done.28
  211.0 0.5 collective-permute-start.29
  211.5 1.8 collective-permute-start.30
  213.2 1.6 collective-permute-start.31
  214.9 2.3 %collective-permute-done.29 = bf16[16,16,128]{2,1,0:T(8,128)(2,1)S(1)} collective-permute-done((bf16[16,16,128]{2,1,0:T(8,128)(2,1)S(1)}, bf16[16,16,128]{2,1,0:T(8,128)(2,1)S(1)}, u32[]{:S(2)}, u32[]{:S(2)}) %collective-permute-start.29) | collective-permute-done | bytes 65568 | tf_op jit(solution)/shard_map/ppermute | solution.py:223
  217.2 1.3 collective-permute-done.30
  218.6 0.8 copy.14
  (61 shorter events, 2.5 us)
Async XLA Ops:
  6.5 103.9 %all-gather.2.cloned.1.call-start = ((), (), s32[]{:S(2)}) async-start(), calls=%async_computation | async-start | bytes 4718592 | tf_op jit(solution)/shard_map/all_gather | solution.py:243
  11.2 1.7 collective-permute-start
  13.0 9.5 %collective-permute-start.1 = (bf16[2,32,2048]{2,1,0:T(8,128)(2,1)S(1)}, bf16[2,32,2048]{2,1,0:T(8,128)(2,1)S(1)}, u32[]{:S(2)}, u32[]{:S(2)}) collective-permute-start(bf16[2,32,2048]{2,1,0:T(8,128)(2,1)S(1)} %get-tuple-element.80), channel_id=1, source_target_pairs={{0,16},{1,17},{2,18},{3,19},{4,20},{5,21},{6,22},{7,23},{8,24},{9,... | collective-permute-start | bytes 786440 | tf_op jit(solution)/shard_map/ppermute | solution.py:223
  30.0 40.6 %copy-start.1 = (bf16[24,32,512]{2,1,0:T(8,128)(2,1)}, bf16[24,32,512]{2,1,0:T(8,128)(2,1)S(1)}, u32[]{:S(2)}) copy-start(bf16[24,32,512]{2,1,0:T(8,128)(2,1)S(1)} %get-tuple-element.42.refs_1_) | copy-start | bytes 2359300
  30.0 19.3 %collective-permute-start.3 = (bf16[24,32,512]{2,1,0:T(8,128)(2,1)}, bf16[24,32,512]{2,1,0:T(8,128)(2,1)}, u32[]{:S(2)}, u32[]{:S(2)}) collective-permute-start(bf16[24,32,512]{2,1,0:T(8,128)(2,1)} %get-tuple-element.78.refs_1_), channel_id=1, source_target_pairs={{0,16},{1,17},{2,18},{3,19},{4,20},{5,21},{6,22},{7,23},{8,24},{9,... | collective-permute-start | bytes 2359304 | tf_op jit(solution)/shard_map/ppermute | solution.py:223
  39.4 11.4 %collective-permute-start.4 = (bf16[24,32,512]{2,1,0:T(8,128)(2,1)}, bf16[24,32,512]{2,1,0:T(8,128)(2,1)}, u32[]{:S(2)}, u32[]{:S(2)}) collective-permute-start(bf16[24,32,512]{2,1,0:T(8,128)(2,1)} %get-tuple-element.78.refs_1_), channel_id=1, source_target_pairs={{0,8},{1,9},{2,10},{3,11},{4,12},{5,13},{6,14},{7,15},{8,0},{9,1},... | collective-permute-start | bytes 2359304 | tf_op jit(solution)/shard_map/ppermute | solution.py:223
  49.3 2.6 %collective-permute-start.5 = (bf16[24,32,512]{2,1,0:T(8,128)(2,1)}, bf16[24,32,512]{2,1,0:T(8,128)(2,1)}, u32[]{:S(2)}, u32[]{:S(2)}) collective-permute-start(bf16[24,32,512]{2,1,0:T(8,128)(2,1)} %collective-permute-done.3.refs_3_), channel_id=1, source_target_pairs={{0,8},{1,9},{2,10},{3,11},{4,12},{5,13},{6,14},{7,15},{8,0},{9,1},... | collective-permute-start | bytes 2359304 | tf_op jit(solution)/shard_map/ppermute | solution.py:223
  49.3 21.3 %collective-permute-start.2 = (bf16[24,32,512]{2,1,0:T(8,128)(2,1)S(1)}, bf16[24,32,512]{2,1,0:T(8,128)(2,1)}, u32[]{:S(2)}, u32[]{:S(2)}) collective-permute-start(bf16[24,32,512]{2,1,0:T(8,128)(2,1)S(1)} %get-tuple-element.42.refs_1_), channel_id=1, source_target_pairs={{0,16},{1,17},{2,18},{3,19},{4,20},{5,21},{6,22},{7,23},{8,24},{9,... | collective-permute-start | bytes 2359304 | tf_op jit(solution)/shard_map/ppermute | solution.py:223
  70.6 2.4 %collective-permute-start.7 = (bf16[24,32,512]{2,1,0:T(8,128)(2,1)S(1)}, bf16[24,32,512]{2,1,0:T(8,128)(2,1)S(1)}, u32[]{:S(2)}, u32[]{:S(2)}) collective-permute-start(bf16[24,32,512]{2,1,0:T(8,128)(2,1)S(1)} %get-tuple-element.42.refs_1_), channel_id=1, source_target_pairs={{0,8},{1,9},{2,10},{3,11},{4,12},{5,13},{6,14},{7,15},{8,0},{9,1},... | collective-permute-start | bytes 2359304 | tf_op jit(solution)/shard_map/ppermute | solution.py:223
  70.8 3.4 %collective-permute-start.8 = (bf16[24,32,512]{2,1,0:T(8,128)(2,1)}, bf16[24,32,512]{2,1,0:T(8,128)(2,1)}, u32[]{:S(2)}, u32[]{:S(2)}) collective-permute-start(bf16[24,32,512]{2,1,0:T(8,128)(2,1)} %collective-permute-done.2.refs_3_), channel_id=1, source_target_pairs={{0,8},{1,9},{2,10},{3,11},{4,12},{5,13},{6,14},{7,15},{8,0},{9,1},... | collective-permute-start | bytes 2359304 | tf_op jit(solution)/shard_map/ppermute | solution.py:223
  71.2 21.8 %copy-start.2 = (bf16[16,32,512]{2,1,0:T(8,128)(2,1)}, bf16[16,32,512]{2,1,0:T(8,128)(2,1)S(1)}, u32[]{:S(2)}) copy-start(bf16[16,32,512]{2,1,0:T(8,128)(2,1)S(1)} %slice.90.refs_1_) | copy-start | bytes 1572868
  71.2 22.2 %copy-start.3 = (s32[8,2,2]{0,2,1:T(2,128)S(1)}, s32[8,2,2]{0,2,1:T(2,128)}, u32[]{:S(2)}) copy-start(s32[8,2,2]{0,2,1:T(2,128)} %param.5) | copy-start | bytes 388
  71.2 21.6 %collective-permute-start.6 = (bf16[16,32,512]{2,1,0:T(8,128)(2,1)S(1)}, bf16[16,32,512]{2,1,0:T(8,128)(2,1)S(1)}, u32[]{:S(2)}, u32[]{:S(2)}) collective-permute-start(bf16[16,32,512]{2,1,0:T(8,128)(2,1)S(1)} %slice.90.refs_1_), channel_id=1, source_target_pairs={{0,16},{1,17},{2,18},{3,19},{4,20},{5,21},{6,22},{7,23},{8,24},{9,... | collective-permute-start | bytes 1572872 | tf_op jit(solution)/shard_map/ppermute | solution.py:223
  72.9 0.9 copy-start.4
  92.8 2.7 %copy-start.5 = (bf16[16,32,512]{2,1,0:T(8,128)(2,1)}, bf16[16,32,512]{2,1,0:T(8,128)(2,1)S(1)}, u32[]{:S(2)}) copy-start(bf16[16,32,512]{2,1,0:T(8,128)(2,1)S(1)} %collective-permute-done.6.refs_3_) | copy-start | bytes 1572868
  92.8 2.0 collective-permute-start.10
  93.0 2.5 %collective-permute-start.9 = (bf16[16,32,512]{2,1,0:T(8,128)(2,1)S(1)}, bf16[16,32,512]{2,1,0:T(8,128)(2,1)S(1)}, u32[]{:S(2)}, u32[]{:S(2)}) collective-permute-start(bf16[16,32,512]{2,1,0:T(8,128)(2,1)S(1)} %slice.90.refs_1_), channel_id=1, source_target_pairs={{0,8},{1,9},{2,10},{3,11},{4,12},{5,13},{6,14},{7,15},{8,0},{9,1},... | collective-permute-start | bytes 1572872 | tf_op jit(solution)/shard_map/ppermute | solution.py:223
  94.8 0.8 copy-start.6
  95.6 0.8 copy-start.7
  127.2 3.6 %collective-permute-start.11 = (bf16[2,2,4,24,16,128]{5,4,3,2,1,0:T(8,128)(2,1)}, bf16[2,2,4,24,16,128]{5,4,3,2,1,0:T(8,128)(2,1)S(1)}, u32[]{:S(2)}, u32[]{:S(2)}) collective-permute-start(bf16[2,2,4,24,16,128]{5,4,3,2,1,0:T(8,128)(2,1)} %get-tuple-element.50), channel_id=1, source_target_pairs={{0,8},{1,9},{2,10},{3,11},{4,12},{5,13},{6,14},{7,15},{8,0},{9,1},... | collective-permute-start | bytes 4718600 | tf_op jit(solution)/shard_map/ppermute | solution.py:223
  150.5 3.9 %collective-permute-start.18 = (bf16[2,2,4,24,16,128]{5,4,3,2,1,0:T(8,128)(2,1)}, bf16[2,2,4,24,16,128]{5,4,3,2,1,0:T(8,128)(2,1)S(1)}, u32[]{:S(2)}, u32[]{:S(2)}) collective-permute-start(bf16[2,2,4,24,16,128]{5,4,3,2,1,0:T(8,128)(2,1)} %get-tuple-element.58), channel_id=1, source_target_pairs={{0,8},{1,9},{2,10},{3,11},{4,12},{5,13},{6,14},{7,15},{8,0},{9,1},... | collective-permute-start | bytes 4718600 | tf_op jit(solution)/shard_map/ppermute | solution.py:223
  150.6 19.0 %collective-permute-start.12 = (bf16[4,24,16,128]{3,2,1,0:T(8,128)(2,1)}, bf16[4,24,16,128]{3,2,1,0:T(8,128)(2,1)}, u32[]{:S(2)}, u32[]{:S(2)}) collective-permute-start(bf16[4,24,16,128]{3,2,1,0:T(8,128)(2,1)} %get-tuple-element.52), channel_id=1, source_target_pairs={{0,1},{1,0},{2,3},{3,2},{4,5},{5,4},{6,7},{7,6},{8,9},{9,8},{10,11... | collective-permute-start | bytes 1179656 | tf_op jit(solution)/shard_map/ppermute | solution.py:223
  152.1 17.6 %collective-permute-start.13 = (bf16[4,24,16,128]{3,2,1,0:T(8,128)(2,1)}, bf16[4,24,16,128]{3,2,1,0:T(8,128)(2,1)}, u32[]{:S(2)}, u32[]{:S(2)}) collective-permute-start(bf16[4,24,16,128]{3,2,1,0:T(8,128)(2,1)} %get-tuple-element.53), channel_id=1, source_target_pairs={{0,16},{1,17},{2,18},{3,19},{4,20},{5,21},{6,22},{7,23},{8,24},{9,... | collective-permute-start | bytes 1179656 | tf_op jit(solution)/shard_map/ppermute | solution.py:223
  154.3 18.1 %collective-permute-start.14 = (bf16[4,24,16,128]{3,2,1,0:T(8,128)(2,1)S(1)}, bf16[4,24,16,128]{3,2,1,0:T(8,128)(2,1)}, u32[]{:S(2)}, u32[]{:S(2)}) collective-permute-start(bf16[4,24,16,128]{3,2,1,0:T(8,128)(2,1)S(1)} %get-tuple-element.54), channel_id=1, source_target_pairs={{0,17},{1,16},{2,19},{3,18},{4,21},{5,20},{6,23},{7,22},{8,25},{9,... | collective-permute-start | bytes 1179656 | tf_op jit(solution)/shard_map/ppermute | solution.py:223
  169.7 17.3 %collective-permute-start.25 = (bf16[2,2,4,16,16,128]{5,4,3,2,1,0:T(8,128)(2,1)}, bf16[2,2,4,16,16,128]{5,4,3,2,1,0:T(8,128)(2,1)S(1)}, u32[]{:S(2)}, u32[]{:S(2)}) collective-permute-start(bf16[2,2,4,16,16,128]{5,4,3,2,1,0:T(8,128)(2,1)} %get-tuple-element.66), channel_id=1, source_target_pairs={{0,8},{1,9},{2,10},{3,11},{4,12},{5,13},{6,14},{7,15},{8,0},{9,1},... | collective-permute-start | bytes 3145736 | tf_op jit(solution)/shard_map/ppermute | solution.py:223
  169.7 17.3 %copy-start = (bf16[2,2,4,16,16,128]{5,4,3,2,1,0:T(8,128)(2,1)S(1)}, bf16[2,2,4,16,16,128]{5,4,3,2,1,0:T(8,128)(2,1)}, u32[]{:S(2)}) copy-start(bf16[2,2,4,16,16,128]{5,4,3,2,1,0:T(8,128)(2,1)} %get-tuple-element.65) | copy-start | bytes 3145732
  173.9 7.6 %collective-permute-start.15 = (bf16[24,16,128]{2,1,0:T(8,128)(2,1)S(1)}, bf16[24,16,128]{2,1,0:T(8,128)(2,1)S(1)}, u32[]{:S(2)}, u32[]{:S(2)}) collective-permute-start(bf16[24,16,128]{2,1,0:T(8,128)(2,1)S(1)} %get-tuple-element.84), channel_id=1, source_target_pairs={{0,2},{1,3},{2,4},{3,5},{4,6},{5,7},{6,0},{7,1},{8,10},{9,11},{10,... | collective-permute-start | bytes 294920 | tf_op jit(solution)/shard_map/ppermute | solution.py:223
  175.5 9.0 %collective-permute-start.16 = (bf16[24,16,128]{2,1,0:T(8,128)(2,1)S(1)}, bf16[24,16,128]{2,1,0:T(8,128)(2,1)S(1)}, u32[]{:S(2)}, u32[]{:S(2)}) collective-permute-start(bf16[24,16,128]{2,1,0:T(8,128)(2,1)S(1)} %get-tuple-element.86), channel_id=1, source_target_pairs={{0,4},{1,5},{2,6},{3,7},{4,0},{5,1},{6,2},{7,3},{8,12},{9,13},{10,... | collective-permute-start | bytes 294920 | tf_op jit(solution)/shard_map/ppermute | solution.py:223
  178.1 8.8 %collective-permute-start.17 = (bf16[24,16,128]{2,1,0:T(8,128)(2,1)S(1)}, bf16[24,16,128]{2,1,0:T(8,128)(2,1)S(1)}, u32[]{:S(2)}, u32[]{:S(2)}) collective-permute-start(bf16[24,16,128]{2,1,0:T(8,128)(2,1)S(1)} %get-tuple-element.85), channel_id=1, source_target_pairs={{0,6},{1,7},{2,0},{3,1},{4,2},{5,3},{6,4},{7,5},{8,14},{9,15},{10,... | collective-permute-start | bytes 294920 | tf_op jit(solution)/shard_map/ppermute | solution.py:223
  179.7 14.0 %collective-permute-start.19 = (bf16[4,24,16,128]{3,2,1,0:T(8,128)(2,1)}, bf16[4,24,16,128]{3,2,1,0:T(8,128)(2,1)S(1)}, u32[]{:S(2)}, u32[]{:S(2)}) collective-permute-start(bf16[4,24,16,128]{3,2,1,0:T(8,128)(2,1)} %get-tuple-element.60), channel_id=1, source_target_pairs={{0,1},{1,0},{2,3},{3,2},{4,5},{5,4},{6,7},{7,6},{8,9},{9,8},{10,11... | collective-permute-start | bytes 1179656 | tf_op jit(solution)/shard_map/ppermute | solution.py:223
  181.5 19.4 %collective-permute-start.20 = (bf16[4,24,16,128]{3,2,1,0:T(8,128)(2,1)}, bf16[4,24,16,128]{3,2,1,0:T(8,128)(2,1)S(1)}, u32[]{:S(2)}, u32[]{:S(2)}) collective-permute-start(bf16[4,24,16,128]{3,2,1,0:T(8,128)(2,1)} %get-tuple-element.61), channel_id=1, source_target_pairs={{0,16},{1,17},{2,18},{3,19},{4,20},{5,21},{6,22},{7,23},{8,24},{9,... | collective-permute-start | bytes 1179656 | tf_op jit(solution)/shard_map/ppermute | solution.py:223
  184.5 18.3 %collective-permute-start.21 = (bf16[4,24,16,128]{3,2,1,0:T(8,128)(2,1)}, bf16[4,24,16,128]{3,2,1,0:T(8,128)(2,1)S(1)}, u32[]{:S(2)}, u32[]{:S(2)}) collective-permute-start(bf16[4,24,16,128]{3,2,1,0:T(8,128)(2,1)} %get-tuple-element.62), channel_id=1, source_target_pairs={{0,17},{1,16},{2,19},{3,18},{4,21},{5,20},{6,23},{7,22},{8,25},{9,... | collective-permute-start | bytes 1179656 | tf_op jit(solution)/shard_map/ppermute | solution.py:223
  187.2 19.0 %collective-permute-start.26 = (bf16[4,16,16,128]{3,2,1,0:T(8,128)(2,1)S(1)}, bf16[4,16,16,128]{3,2,1,0:T(8,128)(2,1)S(1)}, u32[]{:S(2)}, u32[]{:S(2)}) collective-permute-start(bf16[4,16,16,128]{3,2,1,0:T(8,128)(2,1)S(1)} %get-tuple-element.75), channel_id=1, source_target_pairs={{0,1},{1,0},{2,3},{3,2},{4,5},{5,4},{6,7},{7,6},{8,9},{9,8},{10,11... | collective-permute-start | bytes 786440 | tf_op jit(solution)/shard_map/ppermute | solution.py:223
  187.8 21.3 %collective-permute-start.27 = (bf16[4,16,16,128]{3,2,1,0:T(8,128)(2,1)S(1)}, bf16[4,16,16,128]{3,2,1,0:T(8,128)(2,1)S(1)}, u32[]{:S(2)}, u32[]{:S(2)}) collective-permute-start(bf16[4,16,16,128]{3,2,1,0:T(8,128)(2,1)S(1)} %get-tuple-element.77), channel_id=1, source_target_pairs={{0,16},{1,17},{2,18},{3,19},{4,20},{5,21},{6,22},{7,23},{8,24},{9,... | collective-permute-start | bytes 786440 | tf_op jit(solution)/shard_map/ppermute | solution.py:223
  193.7 17.0 %collective-permute-start.28 = (bf16[4,16,16,128]{3,2,1,0:T(8,128)(2,1)S(1)}, bf16[4,16,16,128]{3,2,1,0:T(8,128)(2,1)S(1)}, u32[]{:S(2)}, u32[]{:S(2)}) collective-permute-start(bf16[4,16,16,128]{3,2,1,0:T(8,128)(2,1)S(1)} %get-tuple-element.76), channel_id=1, source_target_pairs={{0,17},{1,16},{2,19},{3,18},{4,21},{5,20},{6,23},{7,22},{8,25},{9,... | collective-permute-start | bytes 786440 | tf_op jit(solution)/shard_map/ppermute | solution.py:223
  203.0 10.2 %collective-permute-start.22 = (bf16[24,16,128]{2,1,0:T(8,128)(2,1)S(1)}, bf16[24,16,128]{2,1,0:T(8,128)(2,1)S(1)}, u32[]{:S(2)}, u32[]{:S(2)}) collective-permute-start(bf16[24,16,128]{2,1,0:T(8,128)(2,1)S(1)} %get-tuple-element.87), channel_id=1, source_target_pairs={{0,2},{1,3},{2,4},{3,5},{4,6},{5,7},{6,0},{7,1},{8,10},{9,11},{10,... | collective-permute-start | bytes 294920 | tf_op jit(solution)/shard_map/ppermute | solution.py:223
  205.9 8.9 %collective-permute-start.23 = (bf16[24,16,128]{2,1,0:T(8,128)(2,1)S(1)}, bf16[24,16,128]{2,1,0:T(8,128)(2,1)S(1)}, u32[]{:S(2)}, u32[]{:S(2)}) collective-permute-start(bf16[24,16,128]{2,1,0:T(8,128)(2,1)S(1)} %get-tuple-element.89), channel_id=1, source_target_pairs={{0,4},{1,5},{2,6},{3,7},{4,0},{5,1},{6,2},{7,3},{8,12},{9,13},{10,... | collective-permute-start | bytes 294920 | tf_op jit(solution)/shard_map/ppermute | solution.py:223
  206.3 8.6 %collective-permute-start.24 = (bf16[24,16,128]{2,1,0:T(8,128)(2,1)S(1)}, bf16[24,16,128]{2,1,0:T(8,128)(2,1)S(1)}, u32[]{:S(2)}, u32[]{:S(2)}) collective-permute-start(bf16[24,16,128]{2,1,0:T(8,128)(2,1)S(1)} %get-tuple-element.88), channel_id=1, source_target_pairs={{0,6},{1,7},{2,0},{3,1},{4,2},{5,3},{6,4},{7,5},{8,14},{9,15},{10,... | collective-permute-start | bytes 294920 | tf_op jit(solution)/shard_map/ppermute | solution.py:223
  211.0 6.2 %collective-permute-start.29 = (bf16[16,16,128]{2,1,0:T(8,128)(2,1)S(1)}, bf16[16,16,128]{2,1,0:T(8,128)(2,1)S(1)}, u32[]{:S(2)}, u32[]{:S(2)}) collective-permute-start(bf16[16,16,128]{2,1,0:T(8,128)(2,1)S(1)} %get-tuple-element.90), channel_id=1, source_target_pairs={{0,2},{1,3},{2,4},{3,5},{4,6},{5,7},{6,0},{7,1},{8,10},{9,11},{10,... | collective-permute-start | bytes 196616 | tf_op jit(solution)/shard_map/ppermute | solution.py:223
  211.5 7.0 %collective-permute-start.30 = (bf16[16,16,128]{2,1,0:T(8,128)(2,1)S(1)}, bf16[16,16,128]{2,1,0:T(8,128)(2,1)S(1)}, u32[]{:S(2)}, u32[]{:S(2)}) collective-permute-start(bf16[16,16,128]{2,1,0:T(8,128)(2,1)S(1)} %get-tuple-element.92), channel_id=1, source_target_pairs={{0,4},{1,5},{2,6},{3,7},{4,0},{5,1},{6,2},{7,3},{8,12},{9,13},{10,... | collective-permute-start | bytes 196616 | tf_op jit(solution)/shard_map/ppermute | solution.py:223
  213.2 5.2 %collective-permute-start.31 = (bf16[16,16,128]{2,1,0:T(8,128)(2,1)S(1)}, bf16[16,16,128]{2,1,0:T(8,128)(2,1)S(1)}, u32[]{:S(2)}, u32[]{:S(2)}) collective-permute-start(bf16[16,16,128]{2,1,0:T(8,128)(2,1)S(1)} %get-tuple-element.91), channel_id=1, source_target_pairs={{0,6},{1,7},{2,0},{3,1},{4,2},{5,3},{6,4},{7,5},{8,14},{9,15},{10,... | collective-permute-start | bytes 196616 | tf_op jit(solution)/shard_map/ppermute | solution.py:223
Sparse Core Ops, SparseCore 0:
  29.1 74.2 all-gather.1
